TPU v7x, 128 devices: a whole 4x4x4 slice. The times are simulated.
128 devices in a mesh: facet: 16 (over x, z_lo, core), col: 8 (over z_hi, y).
Axes of the slice: x: 4, y: 4, z: 4 (z_hi: 2, z_lo: 2; z = z_hi * 2 + z_lo), core: 2. Of those that a mesh axis runs over, the one named last changes fastest.
Arguments:
- strips: float32 [16, 2, 384, 2048], P('facet', None, 'col'), may hold values from -6 to 6
- sub_offset: int32 [8, 16], replicated, may hold values from 0 to 2047
- uv_cells: int32 [8, 16, 2, 128], P('col', 'facet'), may hold values from 0 to 255
- measured: float32 [8, 16, 2, 128], P('col', 'facet'), may hold values from -6 to 6
Outputs:
- dirty_image: float32 [16, 2, 384, 2048], P('facet', None, 'col')
- residual_vis: float32 [8, 16, 2, 128], P('col', 'facet')
All inputs are finite; a program needn't handle non-finite values.
Results may differ from a plain program's by a relative error of at most 0.0003.
Values sent between devices are 32-bit elements; how exact they have to be, the bound alone decides.
No kernel may reach another device: no remote copies, remote signals or barrier semaphores. Data moves between devices by JAX's collectives and lax.ppermute only.
A program may use at most 64 MiB of HBM per device.

v0:
```python
import math

import jax
import jax.numpy as jnp
from jax import lax
from jax.sharding import PartitionSpec as P

SUBGRID_SIZE = 256


def complex_product(ar, ai, br, bi):
    high_precision = lax.Precision.HIGHEST
    rr = jnp.dot(ar, br, precision=high_precision, preferred_element_type=jnp.float32) - jnp.dot(
        ai, bi, precision=high_precision, preferred_element_type=jnp.float32
    )
    ri = jnp.dot(ar, bi, precision=high_precision, preferred_element_type=jnp.float32) + jnp.dot(
        ai, br, precision=high_precision, preferred_element_type=jnp.float32
    )
    return (rr, ri)


def phase_terms(numer, denom):
    angle = (numer % denom).astype(jnp.float32) * (2.0 * math.pi / denom)
    return (jnp.cos(angle), jnp.sin(angle))


def facet_strip_kernel(grid_offset, strip_width, strip_length):
    rows = jnp.arange(strip_length, dtype=jnp.int32)[:, None]
    cols = jnp.arange(strip_width, dtype=jnp.int32)[None, :]
    cosine, sine = phase_terms(rows * (grid_offset + cols), strip_length)
    norm = 1.0 / math.sqrt(strip_length)
    return (cosine * norm, -sine * norm)


def einsum_hi(form, left, right):
    return jnp.einsum(form, left, right, precision=lax.Precision.HIGHEST)


def subgrid_update(
    kernel_real,
    kernel_imaginary,
    u_coordinates,
    v_coordinates,
    measured_real,
    measured_imaginary,
    facet_count,
):
    strip_width = kernel_real.shape[-1]
    total = strip_width * facet_count
    factor = (facet_count * strip_width * strip_width) ** (-0.25)
    grid_cells = jnp.arange(SUBGRID_SIZE, dtype=jnp.int32)
    cosine, sine = phase_terms(
        grid_cells[:, None] * jnp.arange(total, dtype=jnp.int32)[None, :], total
    )
    ere = factor * cosine
    eim = factor * sine
    ebre = ere.reshape(SUBGRID_SIZE, facet_count, strip_width)
    ebim = eim.reshape(SUBGRID_SIZE, facet_count, strip_width)
    are = einsum_hi("ufk,fkl->ufl", ebre, kernel_real) - einsum_hi(
        "ufk,fkl->ufl", ebim, kernel_imaginary
    )
    aim = einsum_hi("ufk,fkl->ufl", ebre, kernel_imaginary) + einsum_hi(
        "ufk,fkl->ufl", ebim, kernel_real
    )
    sre, sim = complex_product(
        are.reshape(SUBGRID_SIZE, total), aim.reshape(SUBGRID_SIZE, total), ere.T, eim.T
    )
    ucos, usin = phase_terms(u_coordinates[:, None] * grid_cells[None, :], SUBGRID_SIZE)
    v_cosine, v_sine = phase_terms(v_coordinates[:, None] * grid_cells[None, :], SUBGRID_SIZE)
    fure, fuim = (ucos, -usin)
    fvre, fvim = (v_cosine, -v_sine)
    tre, tim = complex_product(fure, fuim, sre, sim)
    pred_re = jnp.sum(tre * fvre - tim * fvim, axis=1) / SUBGRID_SIZE
    pred_im = jnp.sum(tre * fvim + tim * fvre, axis=1) / SUBGRID_SIZE
    residual_real = measured_real - pred_re
    residual_imaginary = measured_imaginary - pred_im
    gre = fvre * residual_real[:, None] + fvim * residual_imaginary[:, None]
    gim = fvre * residual_imaginary[:, None] - fvim * residual_real[:, None]
    spre, spim = complex_product(fure.T, -fuim.T, gre, gim)
    bre, bim = complex_product(ere.T, -eim.T, spre, spim)
    bre = bre.reshape(facet_count, strip_width, SUBGRID_SIZE)
    bim = bim.reshape(facet_count, strip_width, SUBGRID_SIZE)
    kernel_phase_real = einsum_hi("fka,afl->fkl", bre, ebre) + einsum_hi("fka,afl->fkl", bim, ebim)
    kernel_phase_imaginary = einsum_hi("fka,afl->fkl", bim, ebre) - einsum_hi(
        "fka,afl->fkl", bre, ebim
    )
    return (residual_real, residual_imaginary, kernel_phase_real, kernel_phase_imaginary)


def body(strips, sub_offset, uv_cells, measured):
    facet_count = lax.axis_size("facet")
    ncol = lax.axis_size("col")
    column = lax.axis_index("col")
    strip_width = strips.shape[2]
    strip_length = strips.shape[3]
    sg_dev = uv_cells.shape[1]
    sg_col = sub_offset.shape[1]
    facet_rows = strip_width * ncol
    left_real = strips[0, 0]
    left_imaginary = strips[0, 1]
    offsets = lax.dynamic_index_in_dim(sub_offset, column, 0, keepdims=False)
    high_precision = lax.Precision.HIGHEST

    def extract(grid_offset):
        vis_real, vis_imaginary = facet_strip_kernel(grid_offset, strip_width, strip_length)
        kernel_real, kernel_imaginary = complex_product(
            left_real, left_imaginary, vis_real, vis_imaginary
        )
        return jnp.concatenate([kernel_real, kernel_imaginary], axis=1)

    contrib = lax.map(extract, offsets).reshape(facet_count, sg_dev, strip_width, 2 * strip_width)
    arrived = lax.all_to_all(contrib, "facet", split_axis=0, concat_axis=0, tiled=True)
    pieces = arrived[:, 0]
    residual_real, residual_imaginary, kernel_phase_real, kernel_phase_imaginary = subgrid_update(
        pieces[:, :, :strip_width],
        pieces[:, :, strip_width:],
        uv_cells[0, 0, 0],
        uv_cells[0, 0, 1],
        measured[0, 0, 0],
        measured[0, 0, 1],
        facet_count,
    )
    residuals = [jnp.stack([residual_real, residual_imaginary])]
    returning = [jnp.concatenate([kernel_phase_real, kernel_phase_imaginary], axis=2)]
    residual_vis = jnp.stack(residuals)[None]
    outgoing = jnp.stack(returning, axis=1)
    back_projection = lax.all_to_all(
        outgoing, "facet", split_axis=0, concat_axis=0, tiled=True
    ).reshape(sg_col, strip_width, 2 * strip_width)
    norm = 1.0 / math.sqrt(facet_rows)

    def add_item(acc, input_arrays):
        grid_offset, piece = input_arrays
        vis_real, vis_imaginary = facet_strip_kernel(grid_offset, strip_width, strip_length)
        phase_real = piece[:, :strip_width]
        phase_imaginary = piece[:, strip_width:]
        right_real = jnp.dot(
            phase_real, vis_real.T, precision=high_precision, preferred_element_type=jnp.float32
        ) + jnp.dot(
            phase_imaginary,
            vis_imaginary.T,
            precision=high_precision,
            preferred_element_type=jnp.float32,
        )
        right_imaginary = jnp.dot(
            phase_imaginary,
            vis_real.T,
            precision=high_precision,
            preferred_element_type=jnp.float32,
        ) - jnp.dot(
            phase_real,
            vis_imaginary.T,
            precision=high_precision,
            preferred_element_type=jnp.float32,
        )
        return ((acc[0] + right_real, acc[1] + right_imaginary), None)

    zero = jnp.zeros((strip_width, strip_length), jnp.float32)
    (right_real, right_imaginary), _ = lax.scan(add_item, (zero, zero), (offsets, back_projection))
    right_real, right_imaginary = (right_real, right_imaginary)
    rows = jnp.arange(lax.axis_size("col") * strip_width, dtype=jnp.int32)
    keys = jnp.arange(strip_width, dtype=jnp.int32) + strip_width * column
    cosine, sine = phase_terms(rows[:, None] * keys[None, :], facet_rows)
    tre, tim = complex_product(cosine * norm, sine * norm, right_real, right_imaginary)
    image = lax.psum_scatter(
        jnp.concatenate([tre, tim], axis=1), "col", scatter_dimension=0, tiled=True
    )
    dirty_image = jnp.stack([image[:, :strip_length], image[:, strip_length:]])[None]
    return (dirty_image, residual_vis)


def solution(mesh):
    return jax.shard_map(
        body,
        mesh=mesh,
        in_specs=(
            P("facet", None, "col", None),
            P(),
            P("col", "facet", None, None),
            P("col", "facet", None, None),
        ),
        out_specs=(P("facet", None, "col", None), P("col", "facet", None, None)),
        check_vma=False,
    )
```

profile of v0, /device:TPU:1, one launch (start us, length us, event | category | flops | bytes accessed | tf_op | source)
XLA Modules:
  0.0 927.2 jit_solution(1982004447034887444)
XLA Ops:
  8.4 326.9 %while.27 = (s32[]{:T(128)}, f32[16,48,96]{2,1,0:T(8,128)}, s32[16]{0:T(128)S(1)}, f32[48,2048]{1,0:T(8,128)S(1)}, f32[48,2048]{1,0:T(8,128)S(1)}, /*index=5*/s32[]{:T(128)}) while((s32[]{:T(128)}, f32[16,48,96]{2,1,0:T(8,128)}, s32[16]{0:T(128)S(1)}, f32[48,2048]{1,0:T(8,128)S(1)}, f32[48,2048]{1,0:T(8,128)S(1)}, /*index=5*/s32[]{:T(128)}) %tuple.61), condition=%wide.region_1.2_spmd, body=%wide.region_0.1_spmd.sunk | while | flops 232596528 | bytes 1672225 | solution.py:111
  335.4 7.2 all-to-all-start
  342.6 8.6 all-to-all-done
  351.4 5.5 fusion.105
  356.9 5.5 fusion.106
  362.4 5.5 convolution_subtract_fusion.4
  376.6 5.7 convolution_add_fusion.4
  401.1 5.5 fusion.101
  406.6 5.5 fusion.100
  417.0 5.5 fusion.104
  427.5 5.5 fusion.103
  433.0 5.5 convolution_add_fusion.5
  438.6 5.5 convolution_subtract_fusion.5
  449.1 8.6 all-to-all-done.1
  457.7 344.7 %while.28 = (s32[]{:T(128)}, f32[48,2048]{1,0:T(8,128)S(1)}, f32[48,2048]{1,0:T(8,128)S(1)}, f32[16,48,96]{2,1,0:T(8,128)S(1)}, s32[16]{0:T(128)S(1)}, /*index=5*/s32[]{:T(128)}, s32[]{:T(128)}) while((s32[]{:T(128)}, f32[48,2048]{1,0:T(8,128)S(1)}, f32[48,2048]{1,0:T(8,128)S(1)}, f32[16,48,96]{2,1,0:T(8,128)S(1)}, ...), condition=%wide.region_5.6_spmd.clone, body=%wide.region_4.5_spmd.clone.sunk | while | flops 233177136 | bytes 3257396 | solution.py:159
  459.1 5.0 fusion.413
  464.2 5.1 fusion.414
  474.2 5.1 fusion.412
  480.6 5.0 fusion.413
  485.7 5.1 fusion.414
  495.8 5.1 fusion.412
  502.2 5.0 fusion.413
  507.2 5.1 fusion.414
  517.3 5.1 fusion.412
  523.7 5.0 fusion.413
  528.7 5.1 fusion.414
  538.8 5.1 fusion.412
  545.2 5.0 fusion.413
  550.2 5.1 fusion.414
  560.3 5.1 fusion.412
  566.7 5.0 fusion.413
  571.8 5.1 fusion.414
  581.9 5.1 fusion.412
  588.3 5.0 fusion.413
  593.3 5.1 fusion.414
  603.4 5.1 fusion.412
  609.8 5.0 fusion.413
  614.8 5.1 fusion.414
  624.9 5.1 fusion.412
  631.3 5.0 fusion.413
  636.3 5.1 fusion.414
  646.4 5.1 fusion.412
  652.8 5.0 fusion.413
  657.9 5.1 fusion.414
  668.0 5.1 fusion.412
  674.4 5.0 fusion.413
  679.4 5.1 fusion.414
  689.5 5.1 fusion.412
  695.9 5.0 fusion.413
  700.9 5.1 fusion.414
  711.0 5.1 fusion.412
  717.4 5.0 fusion.413
  722.4 5.1 fusion.414
  732.5 5.1 fusion.412
  738.9 5.0 fusion.413
  744.0 5.1 fusion.414
  754.1 5.1 fusion.412
  760.5 5.0 fusion.413
  765.5 5.1 fusion.414
  775.6 5.1 fusion.412
  782.0 5.0 fusion.413
  787.0 5.1 fusion.414
  797.1 5.1 fusion.412
  819.5 98.4 %reduce-scatter.2.cloned.1.call-done = f32[48,4096]{1,0:T(8,128)} async-done(((f32[384,4096]{1,0:T(8,128)}), f32[48,4096]{1,0:T(8,128)}) %reduce-scatter.2.cloned.1.call-update) | async-done | bytes 786448 | tf_op jit(solution)/shard_map/reduce_scatter | solution.py:165
  (219 shorter events, 489.3 us)
Async XLA Ops:
  7.2 1.2 copy-start
  8.4 334.2 %copy-start.2 = (s32[1,1,2,128]{3,2,1,0:T(2,128)S(1)}, s32[1,1,2,128]{3,2,1,0:T(2,128)}, u32[]{:S(2)}) copy-start(s32[1,1,2,128]{3,2,1,0:T(2,128)} %param.10) | copy-start | bytes 3076
  335.4 15.8 %all-to-all-start = ((f32[16,1,48,96]{3,2,1,0:T(8,128)}), f32[16,1,48,96]{3,2,1,0:T(8,128)S(1)}, u32[]{:S(2)}, u32[]{:S(2)}) async-start(f32[16,1,48,96]{3,2,1,0:T(8,128)} %bitcast.10), calls=%async_computation | async-start | bytes 786432 | tf_op jit(solution)/shard_map/all_to_all | solution.py:112
  386.6 8.6 copy-start.1
  445.0 12.7 %all-to-all-start.1 = ((f32[16,1,48,96]{3,2,1,0:T(8,128)}), f32[16,1,48,96]{3,2,1,0:T(8,128)S(1)}, u32[]{:S(2)}, u32[]{:S(2)}) async-start(f32[16,1,48,96]{3,2,1,0:T(8,128)} %maximum_bitcast_fusion.2), calls=%async_computation.1 | async-start | bytes 786432 | tf_op jit(solution)/shard_map/all_to_all | solution.py:127
  449.1 468.9 %reduce-scatter.2.cloned.1.call-start = ((), (), s32[]{:S(2)}) async-start(), calls=%async_computation.3 | async-start | bytes 7077888 | tf_op jit(solution)/shard_map/reduce_scatter | solution.py:165
Sparse Core Ops, SparseCore 0:
  819.1 98.8 reduce-scatter.1
where the time goes:
time: 941 us; the launch traced here: 927 us
  matrix products  724 us (77%)
  waiting for transfers between devices  116 us (12%)
  other arithmetic  37 us (4%)
  local copies, waits for them, and re-layouts  22.3 us (2%)
  between operations  14.8 us (2%)
  starting transfers between devices  11.3 us (1%)
    reduce_scatter x1, waiting for transfers between devices, body(): lax.psum_scatter(jnp.concatenate([tre, tim], axis=1), 'col', scatter_dime...  98.4 us
    dot_general x21, matrix products, complex_product(): jnp.dot(ai, br, precision=high_precision, preferred_element_type=jnp.floa...  89.4 us
    dot_general x21, matrix products, complex_product(): jnp.dot(ar, bi, precision=high_precision, preferred_element_type=jnp.floa...  89.3 us
    dot_general x21, matrix products, complex_product(): jnp.dot(ar, br, precision=high_precision, preferred_element_type=jnp.floa...  88.9 us
    dot_general x21, matrix products, complex_product(): jnp.dot(ai, bi, precision=high_precision, preferred_element_type=jnp.floa...  88.9 us
    dot_general x16, matrix products, add_item(): jnp.dot(phase_imaginary, vis_imaginary.T, precision=high_precision, prefe...  81.6 us
    dot_general x16, matrix products, add_item(): jnp.dot(phase_real, vis_imaginary.T, precision=high_precision, preferred_...  81 us
    dot_general x16, matrix products, add_item(): jnp.dot(phase_imaginary, vis_real.T, precision=high_precision, preferred_...  80.5 us
  transfers between devices with their start and end apart: 3, of which 3 were waited for; matrix products, arithmetic and copies ran while one was open for 0% of the time, Pallas kernels for 0%

commit v1 on v0

v1 whole, which is shorter than its diff:
```python
import math

import jax
import jax.numpy as jnp
import ml_dtypes
import numpy as np
from jax import lax
from jax.experimental import pallas as pl
from jax.experimental.pallas import tpu as pltpu
from jax.sharding import PartitionSpec as P

SUBGRID = 256
WIDTH = 48
LENGTH = 2048
FACETS = 16
COLS = 8
ROWS = 384
PADDED = LENGTH + WIDTH
TOTAL = FACETS * WIDTH
F32 = jnp.float32
BF16 = jnp.bfloat16


def split_np(x):
    x = np.asarray(x, np.float32)
    hi = x.astype(ml_dtypes.bfloat16)
    lo = (x - hi.astype(np.float32)).astype(ml_dtypes.bfloat16)
    return hi, lo


def split(x):
    hi = x.astype(BF16)
    lo = (x - hi.astype(F32)).astype(BF16)
    return hi, lo


def dot(a, b, transposed=False):
    dims = (((1,), (1 if transposed else 0,)), ((), ()))
    return lax.dot_general(a, b, dims, preferred_element_type=F32)


def dot3(a, b, transposed=False):
    (ah, al), (bh, bl) = a, b
    return dot(ah, bh, transposed) + dot(ah, bl, transposed) + dot(al, bh, transposed)


def fft_list(xs, sign):
    n = len(xs)
    if n == 1:
        return xs
    even = fft_list(xs[0::2], sign)
    odd = fft_list(xs[1::2], sign)
    half = n // 2
    out = [None] * n
    for k in range(half):
        (er, ei), (r, i) = even[k], odd[k]
        if k == 0:
            tr, ti = r, i
        elif 4 * k == n:
            tr, ti = -sign * i, sign * r
        elif 8 * k == n:
            h = math.sqrt(0.5)
            tr, ti = h * (r - sign * i), h * (i + sign * r)
        elif 8 * k == 3 * n:
            h = math.sqrt(0.5)
            tr, ti = -h * (r + sign * i), h * (sign * r - i)
        else:
            c = math.cos(2 * math.pi * k / n)
            s = sign * math.sin(2 * math.pi * k / n)
            tr, ti = c * r - s * i, s * r + c * i
        out[k] = (er + tr, ei + ti)
        out[k + half] = (er - tr, ei - ti)
    return out


def tables():
    lane = np.arange(128)
    beta = np.arange(16)[:, None]
    ang = 2 * np.pi * ((lane[None, :] * beta) % LENGTH) / LENGTH
    norm = 1 / math.sqrt(LENGTH)
    twiddle = (np.stack([np.cos(ang), np.sin(ang)]) * norm).astype(np.float32)
    ang = 2 * np.pi * ((lane[:, None] * lane[None, :]) % 128) / 128
    cos, sin = np.cos(ang), np.sin(ang)
    forward = np.stack(split_np(np.concatenate([cos, sin], axis=1)))
    backward = np.stack(
        split_np(
            np.concatenate(
                [np.concatenate([cos, sin], axis=1), np.concatenate([-sin, cos], axis=1)], axis=0
            )
        )
    )
    kappa = np.arange(TOTAL).reshape(FACETS, WIDTH, 1) * np.ones((1, 1, 128))
    angle = np.pi * kappa / TOTAL
    rows = np.stack([np.cos(angle), np.sin(angle)], axis=1).astype(np.float32)
    q = float(FACETS * WIDTH * WIDTH) ** (-0.25)
    k = np.arange(WIDTH)
    numer = np.exp(2j * np.pi * (k % 3) / 3) - 1
    a = np.where(k % 3 == 0, 0, -0.5 * q * numer)
    b = np.where(k % 3 == 0, SUBGRID * q, -0.5j * q * numer)
    return twiddle, forward, backward, rows, a, b


def row_coefficients(a, b):
    return np.stack(
        [np.broadcast_to(v[:, None], (WIDTH, 128)) for v in (a.real, a.imag, b.real, b.imag)]
    ).astype(np.float32)


def image_rows(a, b):
    out = np.zeros((COLS, COLS, 2 * WIDTH, 128), ml_dtypes.bfloat16)
    k = np.arange(WIDTH)
    for mine in range(COLS):
        r = WIDTH * mine + np.arange(WIDTH)
        for c in range(COLS):
            phase = np.exp(2j * np.pi * ((r[:, None] * (k + WIDTH * c)[None, :]) % ROWS) / ROWS)
            phase = phase / math.sqrt(ROWS)
            full = np.zeros((WIDTH, 64), complex)
            full[:, :WIDTH] = phase * np.conj(b)[None, :]
            full[:, WIDTH] = phase @ np.conj(a)
            hi, lo = split_np(np.concatenate([full.real, full.imag], axis=0))
            out[mine, c, :, :64] = hi
            out[mine, c, :, 64:] = lo
    return out


def return_coefficients(b):
    lanes = np.arange(128)[None, :]
    sign = np.where(lanes < 64, 1.0, -1.0)
    br = np.broadcast_to(b.real[:, None], (WIDTH, 128))
    bi = b.imag[:, None] * sign
    live = (np.arange(WIDTH) % 3 != 0)[:, None]
    turn = np.where(live, -sign, 0.0)
    return np.stack([br, bi, turn]).astype(np.float32)


def half_turn(cell):
    z = (cell - 128.0) * (math.pi / 256)
    w = z * z
    s = 1.0 / math.factorial(13)
    for n in (11, 9, 7, 5, 3, 1):
        s = s * w + (1.0 if n % 4 == 1 else -1.0) / math.factorial(n)
    c = 1.0 / math.factorial(12)
    for n in (10, 8, 6, 4, 2, 0):
        c = c * w + (1.0 if n % 4 == 0 else -1.0) / math.factorial(n)
    return -(s * z), c


def cotangent(cx, sx, cy, sy, kappa, cell3, threes):
    ratio = (cx * cy + sx * sy) / (sx * cy - cx * sy)
    return jnp.where(threes, jnp.where(kappa == cell3, 1.0, 0.0), ratio)


def extract_kernel(col_ref, offset_ref, x_ref, tw_ref, f_ref, out_ref, mid, spectrum):
    mid[:, WIDTH:64, :] = jnp.zeros((16, 64 - WIDTH, 256), F32)
    for r in range(0, WIDTH, 8):
        xs = [
            (x_ref[0, r : r + 8, 128 * t : 128 * t + 128], x_ref[1, r : r + 8, 128 * t : 128 * t + 128])
            for t in range(16)
        ]
        ys = fft_list(xs, -1.0)
        for beta in range(16):
            yr, yi = ys[beta]
            c = tw_ref[0, beta : beta + 1, :]
            s = tw_ref[1, beta : beta + 1, :]
            mid[beta, r : r + 8, 0:128] = yr * c + yi * s
            mid[beta, r : r + 8, 128:256] = yi * c - yr * s
    left = (f_ref[0], f_ref[1])
    for beta in range(0, 16, 2):
        his, los = [], []
        for b in (beta, beta + 1):
            rh, rl = split(mid[b, :, 0:128])
            ih, il = split(mid[b, :, 128:256])
            his += [jnp.concatenate([rh, ih], axis=1), jnp.concatenate([ih, -rh], axis=1)]
            los += [jnp.concatenate([rl, il], axis=1), jnp.concatenate([il, -rl], axis=1)]
        right = (jnp.concatenate(his, axis=0), jnp.concatenate(los, axis=0))
        freq = dot3(left, right, transposed=True)
        spectrum[pl.ds(beta, 128, stride=16), :] = freq[:, 0:128]
        spectrum[pl.ds(beta + 1, 128, stride=16), :] = freq[:, 128:256]
    spectrum[LENGTH:PADDED, :] = spectrum[0:WIDTH, :]
    column = col_ref[1]
    for s in range(FACETS):
        out_ref[s] = spectrum[pl.ds(offset_ref[column, s], WIDTH), :]


def predict_kernel(k_ref, uv_ref, m_ref, rows_ref, coef_ref, res_ref, send_ref):
    uv = uv_ref[...].astype(F32)
    cy, sy = half_turn(uv)
    iota = lax.broadcasted_iota(jnp.int32, (WIDTH, 128), 0)
    threes = iota % 3 == 0
    kap = iota.astype(F32)
    ar, ai, br, bi = (coef_ref[n] for n in range(4))
    zeros = jnp.zeros((16, 128), F32)

    def one(f, acc):
        cx, sx = rows_ref[f, 0], rows_ref[f, 1]
        base = (f * WIDTH).astype(F32)
        pr, pi = [], []
        for n in range(2):
            cot = cotangent(
                cx, sx, cy[n : n + 1], sy[n : n + 1], kap + base, 3.0 * uv[n : n + 1], threes
            )
            pr.append(ar + br * cot)
            pi.append(ai + bi * cot)
        left = jnp.concatenate([pr[0], zeros, -pi[0], zeros], axis=0)
        right = jnp.concatenate([pi[0], zeros, pr[0], zeros], axis=0)
        mixed = split(jnp.concatenate([left, right], axis=1))
        t = dot3(split(k_ref[f]), mixed)
        tr, ti = t[:, :128], t[:, 128:]
        return (acc[0] + (tr * pr[1] - ti * pi[1]), acc[1] + (tr * pi[1] + ti * pr[1]))

    zero = jnp.zeros((WIDTH, 128), F32)
    sr, si = lax.fori_loop(0, FACETS, one, (zero, zero), unroll=4)
    res = jnp.concatenate(
        [
            m_ref[0:1] - jnp.sum(sr, axis=0, keepdims=True) * (1.0 / SUBGRID),
            m_ref[1:2] - jnp.sum(si, axis=0, keepdims=True) * (1.0 / SUBGRID),
        ],
        axis=0,
    )
    res_ref[...] = res
    send_ref[...] = jnp.broadcast_to(
        jnp.concatenate([res, uv], axis=0)[None], (FACETS * COLS, 4, 128)
    )


def image_kernel(
    pos_ref, offset_ref, got_ref, rows_ref, gamma_ref, coef_ref, tw_ref, b_ref, out_ref, grid, mid, trig
):
    grid[...] = jnp.zeros((PADDED, 128), F32)
    for n in range(2):
        cy, sy = half_turn(got_ref[:, 2 + n, :])
        trig[:, 2 * n, :] = cy
        trig[:, 2 * n + 1, :] = sy
    iota = lax.broadcasted_iota(jnp.int32, (WIDTH, 128), 0)
    threes = iota % 3 == 0
    kap = (iota + WIDTH * pos_ref[0]).astype(F32)
    cx, sx = rows_ref[0, 0], rows_ref[0, 1]
    one = jnp.where(lax.broadcasted_iota(jnp.int32, (16, 128), 0) == 0, 1.0, 0.0)
    one_h = one.astype(BF16)
    zero_h = jnp.zeros((16, 128), BF16)
    block_h = jnp.zeros((64, 128), BF16)
    br, bi, turn = coef_ref[0], coef_ref[1], coef_ref[2]
    group = 4

    def step(g, carry):
        for n in range(group):
            i = g * group + n
            c = i // FACETS
            s = i % FACETS
            got = got_ref[i]
            tr = trig[i]
            rr, ri, u, v = (got[m : m + 1] for m in range(4))
            cu = cotangent(cx, sx, tr[0:1], tr[1:2], kap, 3.0 * u, threes)
            cv = cotangent(cx, sx, tr[2:3], tr[3:4], kap, 3.0 * v, threes)
            uh, ul = split(cu)
            uh = jnp.concatenate([uh, one_h], axis=0)
            ul = jnp.concatenate([ul, zero_h], axis=0)
            right = jnp.concatenate(
                [jnp.concatenate([uh, ul], axis=1), jnp.concatenate([uh, block_h], axis=1)], axis=0
            )
            rowsum = dot(gamma_ref[0, c], right)
            rowsum = rowsum[:, :128] + rowsum[:, 128:]
            gr, gi = rowsum[:WIDTH], rowsum[WIDTH:]
            pad = jnp.zeros((64 - WIDTH, 128), F32)
            w = jnp.concatenate([gr * rr - gi * ri, pad, gr * ri + gi * rr, pad], axis=0)
            wh, wl = split(w)
            vh, vl = split(cv)
            vh = jnp.concatenate([vh, one_h], axis=0)
            left = jnp.concatenate(
                [jnp.concatenate([vh, vh], axis=1), jnp.concatenate([vl, jnp.zeros((WIDTH, 128), BF16)], axis=1)],
                axis=0,
            )
            h = dot(left, jnp.concatenate([wh, wl], axis=1), transposed=True)
            total = h[WIDTH : WIDTH + 1]
            h = h[:WIDTH] + h[64 : 64 + WIDTH] + turn * pltpu.roll(total, 64, 1)
            h = br * h + bi * pltpu.roll(h, 64, 1)
            o = offset_ref[c, s]
            grid[pl.ds(o, WIDTH), :] = grid[pl.ds(o, WIDTH), :] + h
        return carry

    lax.fori_loop(0, FACETS * COLS // group, step, 0)
    grid[0:WIDTH, :] = grid[0:WIDTH, :] + grid[LENGTH:PADDED, :]
    right = (b_ref[0], b_ref[1])
    for beta in range(16):
        d = grid[pl.ds(beta, 128, stride=16), :].T
        left = split(jnp.concatenate([d[0:WIDTH], d[64 : 64 + WIDTH]], axis=1))
        t = dot3(left, right)
        yr, yi = t[:, :128], t[:, 128:]
        c = tw_ref[0, beta : beta + 1, :]
        s = tw_ref[1, beta : beta + 1, :]
        mid[beta, :, 0:128] = yr * c - yi * s
        mid[beta, :, 128:256] = yi * c + yr * s
    for r in range(0, WIDTH, 8):
        ys = fft_list(
            [(mid[b, r : r + 8, 0:128], mid[b, r : r + 8, 128:256]) for b in range(16)], 1.0
        )
        for t in range(16):
            out_ref[0, r : r + 8, 128 * t : 128 * t + 128] = ys[t][0]
            out_ref[1, r : r + 8, 128 * t : 128 * t + 128] = ys[t][1]


def params():
    return pltpu.CompilerParams(vmem_limit_bytes=48 << 20)


VM = pltpu.MemorySpace.VMEM
SM = pltpu.MemorySpace.SMEM


def solution(mesh):
    twiddle, forward, backward, rows, a, b = tables()
    coef = row_coefficients(a, b)
    gamma = image_rows(a, b)
    ret = return_coefficients(b)

    def body(strips, sub_offset, uv_cells, measured):
        facet = lax.axis_index("facet")
        column = lax.axis_index("col")
        pos = jnp.stack([facet, column]).astype(jnp.int32)
        vm = pl.BlockSpec(memory_space=VM)
        sm = pl.BlockSpec(memory_space=SM)
        windows = pl.pallas_call(
            extract_kernel,
            out_shape=jax.ShapeDtypeStruct((FACETS, WIDTH, 128), F32),
            in_specs=[sm, sm, vm, vm, vm],
            out_specs=vm,
            scratch_shapes=[pltpu.VMEM((16, 64, 256), F32), pltpu.VMEM((PADDED, 128), F32)],
            compiler_params=params(),
            name="extract",
        )(pos, sub_offset, strips[0], jnp.asarray(twiddle), jnp.asarray(forward))
        arrived = lax.all_to_all(windows, "facet", split_axis=0, concat_axis=0, tiled=True)
        res, send = pl.pallas_call(
            predict_kernel,
            out_shape=(
                jax.ShapeDtypeStruct((2, 128), F32),
                jax.ShapeDtypeStruct((FACETS * COLS, 4, 128), F32),
            ),
            in_specs=[vm] * 5,
            out_specs=(vm, vm),
            compiler_params=params(),
            name="predict",
        )(arrived, uv_cells[0, 0], measured[0, 0], jnp.asarray(rows), jnp.asarray(coef))
        got = lax.all_to_all(send, ("col", "facet"), split_axis=0, concat_axis=0, tiled=True)
        image = pl.pallas_call(
            image_kernel,
            grid_spec=pltpu.PrefetchScalarGridSpec(
                num_scalar_prefetch=2,
                grid=(1,),
                in_specs=[
                    pl.BlockSpec((FACETS * COLS, 4, 128), lambda i, p, o: (0, 0, 0)),
                    pl.BlockSpec((1, 2, WIDTH, 128), lambda i, p, o: (p[0], 0, 0, 0)),
                    pl.BlockSpec((1, COLS, 2 * WIDTH, 128), lambda i, p, o: (p[1], 0, 0, 0)),
                    pl.BlockSpec((3, WIDTH, 128), lambda i, p, o: (0, 0, 0)),
                    pl.BlockSpec((2, 16, 128), lambda i, p, o: (0, 0, 0)),
                    pl.BlockSpec((2, 256, 256), lambda i, p, o: (0, 0, 0)),
                ],
                out_specs=pl.BlockSpec((2, WIDTH, LENGTH), lambda i, p, o: (0, 0, 0)),
                scratch_shapes=[
                    pltpu.VMEM((PADDED, 128), F32),
                    pltpu.VMEM((16, WIDTH, 256), F32),
                    pltpu.VMEM((FACETS * COLS, 4, 128), F32),
                ],
            ),
            out_shape=jax.ShapeDtypeStruct((2, WIDTH, LENGTH), F32),
            compiler_params=params(),
            name="image",
        )(
            pos,
            sub_offset,
            got,
            jnp.asarray(rows),
            jnp.asarray(gamma),
            jnp.asarray(ret),
            jnp.asarray(twiddle),
            jnp.asarray(backward),
        )
        return image[None], res[None, None]

    return jax.shard_map(
        body,
        mesh=mesh,
        in_specs=(
            P("facet", None, "col", None),
            P(),
            P("col", "facet", None, None),
            P("col", "facet", None, None),
        ),
        out_specs=(P("facet", None, "col", None), P("col", "facet", None, None)),
        check_vma=False,
    )
```

time: 941 us -> 69.7 us (0.07); the launches traced: 927 us -> 69.4 us
  matrix products: 724 us -> 0 us
  waiting for transfers between devices: 116 us -> 0 us
  other arithmetic: 37 us -> 0.08 us
  blocking collectives: 0 us -> 34.8 us
  Pallas kernels: 0 us -> 30.2 us
  local copies, waits for them, and re-layouts: 22.3 us -> 3.54 us
  between operations: 14.8 us -> 0.71 us
  starting transfers between devices: 11.3 us -> 0 us
    dot_general x156 -> x0, matrix products: 724 us -> none  [the longest x21 89.4 us: complex_product(): jnp.dot(ai, br, precision=high_precision, preferred_element_type=jnp.floa...]
    reduce_scatter x1 -> x0, waiting for transfers between devices: 98.4 us -> none  [body(): lax.psum_scatter(jnp.concatenate([tre, tim], axis=1), 'col', scatter_dime...]
    all_to_all x0 -> x2, blocking collectives: none -> 34.8 us  [the longest x1 19.1 us: body(): lax.all_to_all(send, ('col', 'facet'), split_axis=0, concat_axis=0, tiled...]
    pallas_call x0 -> x3, Pallas kernels: none -> 30.2 us  [the longest x1 26.7 us: body(): pl.pallas_call(image_kernel, grid_spec=pltpu.PrefetchScalarGridSpec(num_s...]
    add x33 -> x0, other arithmetic: 20.4 us -> none  [the longest x32 20.4 us: facet_strip_kernel(): cosine, sine = phase_terms(rows * (grid_offset + cols), strip_length)]
    dynamic_slice x32 -> x0, local copies, waits for them, and re-layouts: 19.5 us -> none  [body(): lax.map(extract, offsets)]
    all_to_all x2 -> x0, waiting for transfers between devices: 17.1 us -> none  [the longest x1 8.56 us: body(): lax.all_to_all(outgoing, 'facet', split_axis=0, concat_axis=0, tiled=True)]
    all_to_all x2 -> x0, starting transfers between devices: 11.2 us -> none  [the longest x1 7.18 us: body(): lax.all_to_all(contrib, 'facet', split_axis=0, concat_axis=0, tiled=True)]
  transfers between devices with their start and end apart: 3 -> 0, of which waited for: 3 -> 0; matrix products, arithmetic and copies ran while one was open for 0% -> 0% of each run, Pallas kernels for 0% -> 0%
where the time goes in v1:
time: 69.7 us; the launch traced here: 69.4 us
  blocking collectives  34.8 us (50%)
  Pallas kernels  30.2 us (43%)
  local copies, waits for them, and re-layouts  3.54 us (5%)
  between operations  0.71 us (1%)
    pallas_call x1, Pallas kernels, body(): pl.pallas_call(image_kernel, grid_spec=pltpu.PrefetchScalarGridSpec(num_s...  26.7 us
    all_to_all x1, blocking collectives, body(): lax.all_to_all(send, ('col', 'facet'), split_axis=0, concat_axis=0, tiled...  19.1 us
    all_to_all x1, blocking collectives, body(): lax.all_to_all(windows, 'facet', split_axis=0, concat_axis=0, tiled=True)  15.7 us
    unnamed x24, local copies, waits for them, and re-layouts  3.54 us
    pallas_call x1, Pallas kernels, body(): pl.pallas_call(extract_kernel, out_shape=jax.ShapeDtypeStruct((FACETS, WI...  1.82 us
    pallas_call x1, Pallas kernels, body(): pl.pallas_call(predict_kernel, out_shape=(jax.ShapeDtypeStruct((2, 128),...  1.75 us

profile of v1, /device:TPU:1, one launch (start us, length us, event | category | flops | bytes accessed | tf_op | source)
XLA Modules:
  0.0 69.4 jit_solution(155046069306857830)
XLA Ops:
  0.6 0.0 copy-start
  0.6 0.1 pad_add_fusion.col_ref.pos_ref
  0.7 0.0 copy-start.2
  0.7 1.2 %copy-done.2 = f32[1,2,48,2048]{3,2,1,0:T(8,128)S(1)} copy-done((f32[1,2,48,2048]{3,2,1,0:T(8,128)S(1)}, f32[1,2,48,2048]{3,2,1,0:T(8,128)}, u32[]{:S(2)}) %copy-start.2) | copy-done | bytes 786456
  1.9 0.0 copy-start.4
  1.9 0.9 %copy-done.4 = bf16[2,128,256]{2,1,0:T(8,128)(2,1)S(1)} copy-done((bf16[2,128,256]{2,1,0:T(8,128)(2,1)S(1)}, bf16[2,128,256]{2,1,0:T(8,128)(2,1)}, u32[]{:S(2)}) %copy-start.4) | copy-done | bytes 131096
  2.8 0.0 copy-start.7
  2.8 0.7 %copy-done.7 = f32[2,16,128]{2,1,0:T(8,128)S(1)} copy-done((f32[2,16,128]{2,1,0:T(8,128)S(1)}, f32[2,16,128]{2,1,0:T(8,128)}, u32[]{:S(2)}) %copy-start.7) | copy-done | bytes 16408
  3.5 0.0 copy-start.8
  3.5 0.7 copy-done.8
  4.2 0.0 copy-start.5
  4.2 0.0 copy-start.10
  4.2 0.0 copy-start.11
  4.2 1.8 %extract.1 = f32[16,48,128]{2,1,0:T(8,128)S(1)} custom-call(s32[2]{0:T(128)S(1)} %pad_add_fusion.col_ref.pos_ref, s32[8,16]{1,0:T(8,128)S(1)} %copy-done.8, f32[2,48,2048]{2,1,0:T(8,128)S(1)} %bitcast.7, f32[2,16,128]{2,1,0:T(8,128)S(1)} %copy-done.7, bf16[2,128,256]{2,1,0:T(8,128)(2,1)S(1)} %copy-done.4), custom_call_target="tpu_custom_call" | custom-call | tf_op jit(solution)/shard_map/extract/pallas_call | solution.py:322
  6.1 0.0 copy-start.1
  6.1 0.0 copy-start.3
  6.1 0.0 copy-start.6
  6.1 0.0 copy-start.9
  6.1 15.7 %all_to_all.10.k_ref = f32[16,48,128]{2,1,0:T(8,128)S(1)} all-to-all(f32[16,48,128]{2,1,0:T(8,128)S(1)} %extract.1), channel_id=1, replica_groups=mesh['facet'=16,'col'=8] {'facet'}, dimensions={0} | all-to-all | bytes 786432 | tf_op jit(solution)/shard_map/all_to_all | solution.py:331
  21.8 0.0 copy-done
  21.8 0.0 copy-done.5
  21.8 0.0 copy-done.10
  21.8 0.0 copy-done.11
  21.8 1.7 %predict.1 = (f32[2,128]{1,0:T(2,128)}, f32[128,4,128]{2,1,0:T(4,128)S(1)}) custom-call(f32[16,48,128]{2,1,0:T(8,128)S(1)} %all_to_all.10.k_ref, s32[2,128]{1,0:T(2,128)S(1)} %bitcast.8, f32[2,128]{1,0:T(2,128)S(1)} %bitcast.9, f32[16,2,48,128]{3,2,1,0:T(8,128)S(1)} %copy-done, f32[4,48,128]{2,1,0:T(8,128)S(1)} %copy-done.5), custom_call_target="tpu_custom_call" | custom-call | tf_op jit(solution)/shard_map/predict/pallas_call | solution.py:332
  23.6 19.1 %all_to_all.11.got_ref = f32[128,4,128]{2,1,0:T(4,128)S(1)} all-to-all(f32[128,4,128]{2,1,0:T(4,128)S(1)} %get-tuple-element.4), channel_id=1, replica_groups=mesh['facet'=16,'col'=8] {'col','facet'}, dimensions={0} | all-to-all | bytes 524288 | tf_op jit(solution)/shard_map/all_to_all | solution.py:343
  42.7 0.0 copy-done.1
  42.7 0.0 copy-done.3
  42.7 0.0 copy-done.6
  42.7 0.0 copy-done.9
  42.7 26.7 %image.1 = f32[2,48,2048]{2,1,0:T(8,128)} custom-call(s32[2]{0:T(128)S(1)} %pad_add_fusion.col_ref.pos_ref, s32[8,16]{1,0:T(8,128)S(1)} %copy-done.9, f32[128,4,128]{2,1,0:T(4,128)S(1)} %all_to_all.11.got_ref, f32[16,2,48,128]{3,2,1,0:T(8,128)S(1)} %copy-done, bf16[8,8,96,128]{3,2,1,0:T(8,128)(2,1)S(1)} %copy-done.1, f32[3,48,128]{2,1,0:T(8,128)S(1)} %copy-done.6, ...), custom_call_target="tpu_custom_call" | custom-call | tf_op jit(solution)/shard_map/image/pallas_call | solution.py:344
Async XLA Ops:
  0.6 21.2 %copy-start = (f32[16,2,48,128]{3,2,1,0:T(8,128)S(1)}, f32[16,2,48,128]{3,2,1,0:T(8,128)}, u32[]{:S(2)}) copy-start(f32[16,2,48,128]{3,2,1,0:T(8,128)} %constant.25.clone.rows_ref) | copy-start | bytes 2359300
  0.7 1.2 %copy-start.2 = (f32[1,2,48,2048]{3,2,1,0:T(8,128)S(1)}, f32[1,2,48,2048]{3,2,1,0:T(8,128)}, u32[]{:S(2)}) copy-start(f32[1,2,48,2048]{3,2,1,0:T(8,128)} %param.11) | copy-start | bytes 2359300
  1.9 0.9 %copy-start.4 = (bf16[2,128,256]{2,1,0:T(8,128)(2,1)S(1)}, bf16[2,128,256]{2,1,0:T(8,128)(2,1)}, u32[]{:S(2)}) copy-start(bf16[2,128,256]{2,1,0:T(8,128)(2,1)} %constant.24.clone.f_ref) | copy-start | bytes 393220
  2.8 0.7 %copy-start.7 = (f32[2,16,128]{2,1,0:T(8,128)S(1)}, f32[2,16,128]{2,1,0:T(8,128)}, u32[]{:S(2)}) copy-start(f32[2,16,128]{2,1,0:T(8,128)} %constant.23.clone.tw_ref) | copy-start | bytes 49156
  3.5 0.7 copy-start.8
  4.2 17.6 %copy-start.5 = (f32[4,48,128]{2,1,0:T(8,128)S(1)}, f32[4,48,128]{2,1,0:T(8,128)}, u32[]{:S(2)}) copy-start(f32[4,48,128]{2,1,0:T(8,128)} %constant.26.clone.coef_ref) | copy-start | bytes 294916
  4.2 17.6 %copy-start.10 = (s32[1,1,2,128]{3,2,1,0:T(2,128)S(1)}, s32[1,1,2,128]{3,2,1,0:T(2,128)}, u32[]{:S(2)}) copy-start(s32[1,1,2,128]{3,2,1,0:T(2,128)} %param.13) | copy-start | bytes 3076
  4.2 17.6 %copy-start.11 = (f32[1,1,2,128]{3,2,1,0:T(2,128)S(1)}, f32[1,1,2,128]{3,2,1,0:T(2,128)}, u32[]{:S(2)}) copy-start(f32[1,1,2,128]{3,2,1,0:T(2,128)} %param.14) | copy-start | bytes 3076
  6.1 36.6 %copy-start.1 = (bf16[8,8,96,128]{3,2,1,0:T(8,128)(2,1)S(1)}, bf16[8,8,96,128]{3,2,1,0:T(8,128)(2,1)}, u32[]{:S(2)}) copy-start(bf16[8,8,96,128]{3,2,1,0:T(8,128)(2,1)} %constant.27.clone.gamma_ref) | copy-start | bytes 4718596
  6.1 36.6 %copy-start.3 = (bf16[2,256,256]{2,1,0:T(8,128)(2,1)S(1)}, bf16[2,256,256]{2,1,0:T(8,128)(2,1)}, u32[]{:S(2)}) copy-start(bf16[2,256,256]{2,1,0:T(8,128)(2,1)} %constant.29.clone.b_ref) | copy-start | bytes 786436
  6.1 36.6 %copy-start.6 = (f32[3,48,128]{2,1,0:T(8,128)S(1)}, f32[3,48,128]{2,1,0:T(8,128)}, u32[]{:S(2)}) copy-start(f32[3,48,128]{2,1,0:T(8,128)} %constant.28.clone.coef_ref) | copy-start | bytes 221188
  6.1 36.6 %copy-start.9 = (s32[8,16]{1,0:T(8,128)S(1)}, s32[8,16]{1,0:T(8,128)}, u32[]{:S(2)}) copy-start(s32[8,16]{1,0:T(8,128)} %offset_ref.3) | copy-start | bytes 1540

commit v2 on v1

--- a/solution.py
+++ b/solution.py
@@ -14,11 +14,13 @@
 LENGTH = 2048
 FACETS = 16
 COLS = 8
+GROUP = 16
 ROWS = 384
 PADDED = LENGTH + WIDTH
 TOTAL = FACETS * WIDTH
 F32 = jnp.float32
 BF16 = jnp.bfloat16
+ORDER = np.concatenate([np.arange(1, WIDTH, 3), np.arange(2, WIDTH, 3), np.arange(0, WIDTH, 3)])
 
 
 def split_np(x):
@@ -92,12 +94,13 @@
     kappa = np.arange(TOTAL).reshape(FACETS, WIDTH, 1) * np.ones((1, 1, 128))
     angle = np.pi * kappa / TOTAL
     rows = np.stack([np.cos(angle), np.sin(angle)], axis=1).astype(np.float32)
+    live = np.ascontiguousarray(rows[:, :, ORDER[:32]])
     q = float(FACETS * WIDTH * WIDTH) ** (-0.25)
     k = np.arange(WIDTH)
     numer = np.exp(2j * np.pi * (k % 3) / 3) - 1
     a = np.where(k % 3 == 0, 0, -0.5 * q * numer)
     b = np.where(k % 3 == 0, SUBGRID * q, -0.5j * q * numer)
-    return twiddle, forward, backward, rows, a, b
+    return twiddle, forward, backward, rows, live, a, b
 
 
 def row_coefficients(a, b):
@@ -115,22 +118,12 @@
             phase = np.exp(2j * np.pi * ((r[:, None] * (k + WIDTH * c)[None, :]) % ROWS) / ROWS)
             phase = phase / math.sqrt(ROWS)
             full = np.zeros((WIDTH, 64), complex)
-            full[:, :WIDTH] = phase * np.conj(b)[None, :]
+            full[:, :WIDTH] = (phase * np.conj(b)[None, :])[:, ORDER]
             full[:, WIDTH] = phase @ np.conj(a)
             hi, lo = split_np(np.concatenate([full.real, full.imag], axis=0))
             out[mine, c, :, :64] = hi
             out[mine, c, :, 64:] = lo
     return out
-
-
-def return_coefficients(b):
-    lanes = np.arange(128)[None, :]
-    sign = np.where(lanes < 64, 1.0, -1.0)
-    br = np.broadcast_to(b.real[:, None], (WIDTH, 128))
-    bi = b.imag[:, None] * sign
-    live = (np.arange(WIDTH) % 3 != 0)[:, None]
-    turn = np.where(live, -sign, 0.0)
-    return np.stack([br, bi, turn]).astype(np.float32)
 
 
 def half_turn(cell):
@@ -145,14 +138,29 @@
     return -(s * z), c
 
 
+def ratio(cx, sx, cy, sy):
+    return (cx * cy + sx * sy) / (sx * cy - cx * sy)
+
+
 def cotangent(cx, sx, cy, sy, kappa, cell3, threes):
-    ratio = (cx * cy + sx * sy) / (sx * cy - cx * sy)
-    return jnp.where(threes, jnp.where(kappa == cell3, 1.0, 0.0), ratio)
-
-
-def extract_kernel(col_ref, offset_ref, x_ref, tw_ref, f_ref, out_ref, mid, spectrum):
+    return jnp.where(threes, jnp.where(kappa == cell3, 1.0, 0.0), ratio(cx, sx, cy, sy))
+
+
+def extract_kernel(
+    col_ref, offset_hbm, x_hbm, tw_hbm, f_hbm, out_ref, mid, spectrum, offset_ref, x_ref, tw_ref, f_ref, sem
+):
+    copies = [pltpu.make_async_copy(tw_hbm, tw_ref, sem.at[6])]
+    for n in range(6):
+        rows = pl.ds(8 * n, 8)
+        copies.append(pltpu.make_async_copy(x_hbm.at[:, rows, :], x_ref.at[:, rows, :], sem.at[n]))
+    copies.append(pltpu.make_async_copy(f_hbm, f_ref, sem.at[7]))
+    copies.append(pltpu.make_async_copy(offset_hbm, offset_ref, sem.at[8]))
+    for copy in copies:
+        copy.start()
     mid[:, WIDTH:64, :] = jnp.zeros((16, 64 - WIDTH, 256), F32)
+    copies[0].wait()
     for r in range(0, WIDTH, 8):
+        copies[1 + r // 8].wait()
         xs = [
             (x_ref[0, r : r + 8, 128 * t : 128 * t + 128], x_ref[1, r : r + 8, 128 * t : 128 * t + 128])
             for t in range(16)
@@ -164,6 +172,8 @@
             s = tw_ref[1, beta : beta + 1, :]
             mid[beta, r : r + 8, 0:128] = yr * c + yi * s
             mid[beta, r : r + 8, 128:256] = yi * c - yr * s
+    copies[7].wait()
+    copies[8].wait()
     left = (f_ref[0], f_ref[1])
     for beta in range(0, 16, 2):
         his, los = [], []
@@ -224,65 +234,68 @@
 
 
 def image_kernel(
-    pos_ref, offset_ref, got_ref, rows_ref, gamma_ref, coef_ref, tw_ref, b_ref, out_ref, grid, mid, trig
+    pos_ref, offset_ref, got_ref, live_ref, gamma_ref, tw_ref, b_ref, out_ref, grid, mid, trig
 ):
-    grid[...] = jnp.zeros((PADDED, 128), F32)
+    grid[...] = jnp.zeros((3, PADDED, 128), F32)
     for n in range(2):
         cy, sy = half_turn(got_ref[:, 2 + n, :])
         trig[:, 2 * n, :] = cy
         trig[:, 2 * n + 1, :] = sy
-    iota = lax.broadcasted_iota(jnp.int32, (WIDTH, 128), 0)
-    threes = iota % 3 == 0
-    kap = (iota + WIDTH * pos_ref[0]).astype(F32)
-    cx, sx = rows_ref[0, 0], rows_ref[0, 1]
-    one = jnp.where(lax.broadcasted_iota(jnp.int32, (16, 128), 0) == 0, 1.0, 0.0)
-    one_h = one.astype(BF16)
-    zero_h = jnp.zeros((16, 128), BF16)
-    block_h = jnp.zeros((64, 128), BF16)
-    br, bi, turn = coef_ref[0], coef_ref[1], coef_ref[2]
-    group = 4
+    iota = lax.broadcasted_iota(jnp.int32, (16, 128), 0)
+    kap = (iota + 16 * pos_ref[0]).astype(F32)
+    cx, sx = live_ref[0, 0], live_ref[0, 1]
+    one_h = jnp.where(iota == 0, 1.0, 0.0).astype(BF16)
+    none_h = jnp.zeros((32, 128), BF16)
+    pad = jnp.zeros((64 - WIDTH, 128), F32)
+    lanes = lax.broadcasted_iota(jnp.int32, (1, 128), 1)
+    turn = jnp.where(lanes < 64, -1.0, 1.0)
+
+    def parts(cy, sy, cell):
+        hi, lo = split(ratio(cx, sx, cy, sy))
+        hit = jnp.where(kap == cell, 1.0, 0.0).astype(BF16)
+        return jnp.concatenate([hi, hit, one_h], axis=0), lo
 
     def step(g, carry):
-        for n in range(group):
-            i = g * group + n
-            c = i // FACETS
-            s = i % FACETS
-            got = got_ref[i]
-            tr = trig[i]
-            rr, ri, u, v = (got[m : m + 1] for m in range(4))
-            cu = cotangent(cx, sx, tr[0:1], tr[1:2], kap, 3.0 * u, threes)
-            cv = cotangent(cx, sx, tr[2:3], tr[3:4], kap, 3.0 * v, threes)
-            uh, ul = split(cu)
-            uh = jnp.concatenate([uh, one_h], axis=0)
-            ul = jnp.concatenate([ul, zero_h], axis=0)
-            right = jnp.concatenate(
-                [jnp.concatenate([uh, ul], axis=1), jnp.concatenate([uh, block_h], axis=1)], axis=0
-            )
-            rowsum = dot(gamma_ref[0, c], right)
-            rowsum = rowsum[:, :128] + rowsum[:, 128:]
-            gr, gi = rowsum[:WIDTH], rowsum[WIDTH:]
-            pad = jnp.zeros((64 - WIDTH, 128), F32)
+        c = (g * GROUP) // FACETS
+        s = (g * GROUP) % FACETS
+        gam = gamma_ref[0, c]
+        gam = jnp.concatenate([gam, gam[:, :32]], axis=1)
+        gots = [got_ref[g * GROUP + n] for n in range(GROUP)]
+        trigs = [trig[g * GROUP + n] for n in range(GROUP)]
+        us = [parts(t[0:1], t[1:2], r[2:3]) for r, t in zip(gots, trigs)]
+        gs = [dot(gam, jnp.concatenate([h, h, l], axis=0)) for h, l in us]
+        vs = [parts(t[2:3], t[3:4], r[3:4]) for r, t in zip(gots, trigs)]
+        hs = []
+        for n in range(GROUP):
+            rr, ri = gots[n][0:1], gots[n][1:2]
+            gr, gi = gs[n][:WIDTH], gs[n][WIDTH:]
             w = jnp.concatenate([gr * rr - gi * ri, pad, gr * ri + gi * rr, pad], axis=0)
             wh, wl = split(w)
-            vh, vl = split(cv)
-            vh = jnp.concatenate([vh, one_h], axis=0)
+            vh, vl = vs[n]
             left = jnp.concatenate(
-                [jnp.concatenate([vh, vh], axis=1), jnp.concatenate([vl, jnp.zeros((WIDTH, 128), BF16)], axis=1)],
-                axis=0,
+                [jnp.concatenate([vh, vh], axis=1), jnp.concatenate([vl, none_h], axis=1)], axis=0
             )
-            h = dot(left, jnp.concatenate([wh, wl], axis=1), transposed=True)
-            total = h[WIDTH : WIDTH + 1]
-            h = h[:WIDTH] + h[64 : 64 + WIDTH] + turn * pltpu.roll(total, 64, 1)
-            h = br * h + bi * pltpu.roll(h, 64, 1)
-            o = offset_ref[c, s]
-            grid[pl.ds(o, WIDTH), :] = grid[pl.ds(o, WIDTH), :] + h
+            hs.append(dot(left, jnp.concatenate([wh, wl], axis=1), transposed=True))
+        for n in range(GROUP):
+            h = hs[n]
+            total = turn * pltpu.roll(h[WIDTH : WIDTH + 1], 64, 1)
+            o = offset_ref[c, s + n]
+            for m in range(3):
+                add = h[16 * m : 16 * m + 16]
+                if m < 2:
+                    add = add + h[64 + 16 * m : 80 + 16 * m] + total
+                at = pl.ds(o + (m + 1) % 3, 16, stride=3)
+                grid[m, at, :] = grid[m, at, :] + add
         return carry
 
-    lax.fori_loop(0, FACETS * COLS // group, step, 0)
-    grid[0:WIDTH, :] = grid[0:WIDTH, :] + grid[LENGTH:PADDED, :]
+    lax.fori_loop(0, FACETS * COLS // GROUP, step, 0)
+    grid[:, 0:WIDTH, :] = grid[:, 0:WIDTH, :] + grid[:, LENGTH:PADDED, :]
+    q = float(FACETS * WIDTH * WIDTH) ** (-0.25)
     right = (b_ref[0], b_ref[1])
     for beta in range(16):
-        d = grid[pl.ds(beta, 128, stride=16), :].T
+        one, two, nil = (grid[m, pl.ds(beta, 128, stride=16), :] for m in range(3))
+        d = (SUBGRID * q) * nil + (q * math.sqrt(3) / 4) * (one - two)
+        d = (d - (0.75 * q) * turn * pltpu.roll(one + two, 64, 1)).T
         left = split(jnp.concatenate([d[0:WIDTH], d[64 : 64 + WIDTH]], axis=1))
         t = dot3(left, right)
         yr, yi = t[:, :128], t[:, 128:]
@@ -299,6 +312,10 @@
             out_ref[1, r : r + 8, 128 * t : 128 * t + 128] = ys[t][1]
 
 
+def keep(x):
+    return pltpu.with_memory_space_constraint(x, pltpu.MemorySpace.HBM)
+
+
 def params():
     return pltpu.CompilerParams(vmem_limit_bytes=48 << 20)
 
@@ -308,10 +325,9 @@
 
 
 def solution(mesh):
-    twiddle, forward, backward, rows, a, b = tables()
+    twiddle, forward, backward, rows, live, a, b = tables()
     coef = row_coefficients(a, b)
     gamma = image_rows(a, b)
-    ret = return_coefficients(b)
 
     def body(strips, sub_offset, uv_cells, measured):
         facet = lax.axis_index("facet")
@@ -319,15 +335,24 @@
         pos = jnp.stack([facet, column]).astype(jnp.int32)
         vm = pl.BlockSpec(memory_space=VM)
         sm = pl.BlockSpec(memory_space=SM)
+        hbm = pl.BlockSpec(memory_space=pltpu.MemorySpace.HBM)
         windows = pl.pallas_call(
             extract_kernel,
             out_shape=jax.ShapeDtypeStruct((FACETS, WIDTH, 128), F32),
-            in_specs=[sm, sm, vm, vm, vm],
+            in_specs=[sm, hbm, hbm, hbm, hbm],
             out_specs=vm,
-            scratch_shapes=[pltpu.VMEM((16, 64, 256), F32), pltpu.VMEM((PADDED, 128), F32)],
+            scratch_shapes=[
+                pltpu.VMEM((16, 64, 256), F32),
+                pltpu.VMEM((PADDED, 128), F32),
+                pltpu.SMEM((COLS, FACETS), jnp.int32),
+                pltpu.VMEM((2, WIDTH, LENGTH), F32),
+                pltpu.VMEM((2, 16, 128), F32),
+                pltpu.VMEM((2, 128, 256), BF16),
+                pltpu.SemaphoreType.DMA((9,)),
+            ],
             compiler_params=params(),
             name="extract",
-        )(pos, sub_offset, strips[0], jnp.asarray(twiddle), jnp.asarray(forward))
+        )(pos, *(keep(x) for x in (sub_offset, strips[0], jnp.asarray(twiddle), jnp.asarray(forward))))
         arrived = lax.all_to_all(windows, "facet", split_axis=0, concat_axis=0, tiled=True)
         res, send = pl.pallas_call(
             predict_kernel,
@@ -348,15 +373,14 @@
                 grid=(1,),
                 in_specs=[
                     pl.BlockSpec((FACETS * COLS, 4, 128), lambda i, p, o: (0, 0, 0)),
-                    pl.BlockSpec((1, 2, WIDTH, 128), lambda i, p, o: (p[0], 0, 0, 0)),
+                    pl.BlockSpec((1, 2, 32, 128), lambda i, p, o: (p[0], 0, 0, 0)),
                     pl.BlockSpec((1, COLS, 2 * WIDTH, 128), lambda i, p, o: (p[1], 0, 0, 0)),
-                    pl.BlockSpec((3, WIDTH, 128), lambda i, p, o: (0, 0, 0)),
                     pl.BlockSpec((2, 16, 128), lambda i, p, o: (0, 0, 0)),
                     pl.BlockSpec((2, 256, 256), lambda i, p, o: (0, 0, 0)),
                 ],
                 out_specs=pl.BlockSpec((2, WIDTH, LENGTH), lambda i, p, o: (0, 0, 0)),
                 scratch_shapes=[
-                    pltpu.VMEM((PADDED, 128), F32),
+                    pltpu.VMEM((3, PADDED, 128), F32),
                     pltpu.VMEM((16, WIDTH, 256), F32),
                     pltpu.VMEM((FACETS * COLS, 4, 128), F32),
                 ],
@@ -368,9 +392,8 @@
             pos,
             sub_offset,
             got,
-            jnp.asarray(rows),
+            jnp.asarray(live),
             jnp.asarray(gamma),
-            jnp.asarray(ret),
             jnp.asarray(twiddle),
             jnp.asarray(backward),
         )

time: 69.7 us -> 51.7 us (0.74)
  Pallas kernels: 30.2 us -> 15.8 us
  local copies, waits for them, and re-layouts: 3.54 us -> 0.06 us
    pallas_call x1, Pallas kernels: 26.7 us -> 10.9 us  [body(): pl.pallas_call(image_kernel, grid_spec=pltpu.PrefetchScalarGridSpec(num_s...]
    unnamed x24 -> x18, local copies, waits for them, and re-layouts: 3.54 us -> 0.06 us
    pallas_call x1, Pallas kernels: 1.82 us -> 3.12 us  [body(): pl.pallas_call(extract_kernel, out_shape=jax.ShapeDtypeStruct((FACETS, WI...]
where the time goes in v2:
time: 51.7 us; the launch traced here: 51.5 us
  blocking collectives  34.8 us (67%)
  Pallas kernels  15.8 us (31%)
  between operations  0.75 us (1%)
    all_to_all x1, blocking collectives, body(): lax.all_to_all(send, ('col', 'facet'), split_axis=0, concat_axis=0, tiled...  19.1 us
    all_to_all x1, blocking collectives, body(): lax.all_to_all(windows, 'facet', split_axis=0, concat_axis=0, tiled=True)  15.7 us
    pallas_call x1, Pallas kernels, body(): pl.pallas_call(image_kernel, grid_spec=pltpu.PrefetchScalarGridSpec(num_s...  10.9 us
    pallas_call x1, Pallas kernels, body(): pl.pallas_call(extract_kernel, out_shape=jax.ShapeDtypeStruct((FACETS, WI...  3.12 us
    pallas_call x1, Pallas kernels, body(): pl.pallas_call(predict_kernel, out_shape=(jax.ShapeDtypeStruct((2, 128),...  1.77 us

profile of v2, /device:TPU:1, one launch (start us, length us, event | category | flops | bytes accessed | tf_op | source)
XLA Modules:
  0.0 51.5 jit_solution(113613774676620691)
XLA Ops:
  0.6 0.0 copy-start.4
  0.6 0.0 copy-start.1
  0.7 0.0 copy-start.8
  0.7 0.0 copy-start.7
  0.7 0.1 pad_add_fusion.col_ref.pos_ref
  0.8 3.1 %extract.1 = f32[16,48,128]{2,1,0:T(8,128)S(1)} custom-call(s32[2]{0:T(128)S(1)} %pad_add_fusion.col_ref.pos_ref, s32[8,16]{1,0:T(8,128)} %offset_ref.1, f32[2,48,2048]{2,1,0:T(8,128)} %bitcast.9, f32[2,16,128]{2,1,0:T(8,128)} %constant.23.clone.tw_hbm.tw_ref, bf16[2,128,256]{2,1,0:T(8,128)(2,1)} %constant.24.clone.f_hbm), custom_call_target="tpu_custom_call" | custom-call | tf_op jit(solution)/shard_map/extract/pallas_call | solution.py:339
  3.9 0.0 copy-start
  3.9 0.0 copy-start.2
  3.9 0.0 copy-start.3
  3.9 0.0 copy-start.5
  3.9 0.0 copy-start.6
  3.9 15.7 %all_to_all.10.k_ref = f32[16,48,128]{2,1,0:T(8,128)S(1)} all-to-all(f32[16,48,128]{2,1,0:T(8,128)S(1)} %extract.1), channel_id=1, replica_groups=mesh['facet'=16,'col'=8] {'facet'}, dimensions={0} | all-to-all | bytes 786432 | tf_op jit(solution)/shard_map/all_to_all | solution.py:356
  19.6 0.0 copy-done.4
  19.6 0.0 copy-done.1
  19.6 0.0 copy-done.8
  19.6 0.0 copy-done.7
  19.6 1.8 %predict.1 = (f32[2,128]{1,0:T(2,128)}, f32[128,4,128]{2,1,0:T(4,128)S(1)}) custom-call(f32[16,48,128]{2,1,0:T(8,128)S(1)} %all_to_all.10.k_ref, s32[2,128]{1,0:T(2,128)S(1)} %bitcast.7, f32[2,128]{1,0:T(2,128)S(1)} %bitcast.8, f32[16,2,48,128]{3,2,1,0:T(8,128)S(1)} %copy-done.1, f32[4,48,128]{2,1,0:T(8,128)S(1)} %copy-done.4), custom_call_target="tpu_custom_call" | custom-call | tf_op jit(solution)/shard_map/predict/pallas_call | solution.py:357
  21.4 19.1 %all_to_all.11.got_ref = f32[128,4,128]{2,1,0:T(4,128)S(1)} all-to-all(f32[128,4,128]{2,1,0:T(4,128)S(1)} %get-tuple-element.4), channel_id=1, replica_groups=mesh['facet'=16,'col'=8] {'col','facet'}, dimensions={0} | all-to-all | bytes 524288 | tf_op jit(solution)/shard_map/all_to_all | solution.py:368
  40.5 0.0 copy-done
  40.5 0.0 copy-done.2
  40.5 0.0 copy-done.3
  40.5 0.0 copy-done.5
  40.6 0.0 copy-done.6
  40.6 10.9 %image.1 = f32[2,48,2048]{2,1,0:T(8,128)} custom-call(s32[2]{0:T(128)S(1)} %pad_add_fusion.col_ref.pos_ref, s32[8,16]{1,0:T(8,128)S(1)} %copy-done.6, f32[128,4,128]{2,1,0:T(4,128)S(1)} %all_to_all.11.got_ref, f32[16,2,32,128]{3,2,1,0:T(8,128)S(1)} %copy-done.2, bf16[8,8,96,128]{3,2,1,0:T(8,128)(2,1)S(1)} %copy-done, f32[2,16,128]{2,1,0:T(8,128)S(1)} %copy-done.5, ...), custom_call_target="tpu_custom_call" | custom-call | tf_op jit(solution)/shard_map/image/pallas_call | solution.py:369
Async XLA Ops:
  0.6 19.0 %copy-start.4 = (f32[4,48,128]{2,1,0:T(8,128)S(1)}, f32[4,48,128]{2,1,0:T(8,128)}, u32[]{:S(2)}) copy-start(f32[4,48,128]{2,1,0:T(8,128)} %constant.26.clone.coef_ref) | copy-start | bytes 294916
  0.6 19.0 %copy-start.1 = (f32[16,2,48,128]{3,2,1,0:T(8,128)S(1)}, f32[16,2,48,128]{3,2,1,0:T(8,128)}, u32[]{:S(2)}) copy-start(f32[16,2,48,128]{3,2,1,0:T(8,128)} %constant.25.clone.rows_ref) | copy-start | bytes 2359300
  0.7 19.0 %copy-start.8 = (f32[1,1,2,128]{3,2,1,0:T(2,128)S(1)}, f32[1,1,2,128]{3,2,1,0:T(2,128)}, u32[]{:S(2)}) copy-start(f32[1,1,2,128]{3,2,1,0:T(2,128)} %param.14) | copy-start | bytes 3076
  0.7 19.0 %copy-start.7 = (s32[1,1,2,128]{3,2,1,0:T(2,128)S(1)}, s32[1,1,2,128]{3,2,1,0:T(2,128)}, u32[]{:S(2)}) copy-start(s32[1,1,2,128]{3,2,1,0:T(2,128)} %param.13) | copy-start | bytes 3076
  3.9 36.7 %copy-start = (bf16[8,8,96,128]{3,2,1,0:T(8,128)(2,1)S(1)}, bf16[8,8,96,128]{3,2,1,0:T(8,128)(2,1)}, u32[]{:S(2)}) copy-start(bf16[8,8,96,128]{3,2,1,0:T(8,128)(2,1)} %constant.28.clone.gamma_ref) | copy-start | bytes 4718596
  3.9 36.6 %copy-start.2 = (f32[16,2,32,128]{3,2,1,0:T(8,128)S(1)}, f32[16,2,32,128]{3,2,1,0:T(8,128)}, u32[]{:S(2)}) copy-start(f32[16,2,32,128]{3,2,1,0:T(8,128)} %constant.27.clone.live_ref) | copy-start | bytes 1572868
  3.9 36.6 %copy-start.3 = (bf16[2,256,256]{2,1,0:T(8,128)(2,1)S(1)}, bf16[2,256,256]{2,1,0:T(8,128)(2,1)}, u32[]{:S(2)}) copy-start(bf16[2,256,256]{2,1,0:T(8,128)(2,1)} %constant.29.clone.b_ref) | copy-start | bytes 786436
  3.9 36.6 %copy-start.5 = (f32[2,16,128]{2,1,0:T(8,128)S(1)}, f32[2,16,128]{2,1,0:T(8,128)}, u32[]{:S(2)}) copy-start(f32[2,16,128]{2,1,0:T(8,128)} %constant.23.clone.tw_hbm.tw_ref) | copy-start | bytes 49156
  3.9 36.6 %copy-start.6 = (s32[8,16]{1,0:T(8,128)S(1)}, s32[8,16]{1,0:T(8,128)}, u32[]{:S(2)}) copy-start(s32[8,16]{1,0:T(8,128)} %offset_ref.1) | copy-start | bytes 1540

commit v3 on v2

--- a/solution.py
+++ b/solution.py
@@ -14,7 +14,7 @@
 LENGTH = 2048
 FACETS = 16
 COLS = 8
-GROUP = 16
+GROUP = 32
 ROWS = 384
 PADDED = LENGTH + WIDTH
 TOTAL = FACETS * WIDTH
@@ -175,6 +175,7 @@
     copies[7].wait()
     copies[8].wait()
     left = (f_ref[0], f_ref[1])
+    rights = []
     for beta in range(0, 16, 2):
         his, los = [], []
         for b in (beta, beta + 1):
@@ -182,10 +183,11 @@
             ih, il = split(mid[b, :, 128:256])
             his += [jnp.concatenate([rh, ih], axis=1), jnp.concatenate([ih, -rh], axis=1)]
             los += [jnp.concatenate([rl, il], axis=1), jnp.concatenate([il, -rl], axis=1)]
-        right = (jnp.concatenate(his, axis=0), jnp.concatenate(los, axis=0))
-        freq = dot3(left, right, transposed=True)
-        spectrum[pl.ds(beta, 128, stride=16), :] = freq[:, 0:128]
-        spectrum[pl.ds(beta + 1, 128, stride=16), :] = freq[:, 128:256]
+        rights.append((jnp.concatenate(his, axis=0), jnp.concatenate(los, axis=0)))
+    freqs = [dot3(left, right, transposed=True) for right in rights]
+    for beta in range(16):
+        half = 128 * (beta % 2)
+        spectrum[pl.ds(beta, 128, stride=16), :] = freqs[beta // 2][:, half : half + 128]
     spectrum[LENGTH:PADDED, :] = spectrum[0:WIDTH, :]
     column = col_ref[1]
     for s in range(FACETS):
@@ -201,25 +203,27 @@
     ar, ai, br, bi = (coef_ref[n] for n in range(4))
     zeros = jnp.zeros((16, 128), F32)
 
-    def one(f, acc):
+    mixes, others = [], []
+    for f in range(FACETS):
         cx, sx = rows_ref[f, 0], rows_ref[f, 1]
-        base = (f * WIDTH).astype(F32)
         pr, pi = [], []
         for n in range(2):
-            cot = cotangent(
-                cx, sx, cy[n : n + 1], sy[n : n + 1], kap + base, 3.0 * uv[n : n + 1], threes
-            )
+            cell = 3.0 * uv[n : n + 1] - float(f * WIDTH)
+            cot = cotangent(cx, sx, cy[n : n + 1], sy[n : n + 1], kap, cell, threes)
             pr.append(ar + br * cot)
             pi.append(ai + bi * cot)
         left = jnp.concatenate([pr[0], zeros, -pi[0], zeros], axis=0)
         right = jnp.concatenate([pi[0], zeros, pr[0], zeros], axis=0)
-        mixed = split(jnp.concatenate([left, right], axis=1))
-        t = dot3(split(k_ref[f]), mixed)
-        tr, ti = t[:, :128], t[:, 128:]
-        return (acc[0] + (tr * pr[1] - ti * pi[1]), acc[1] + (tr * pi[1] + ti * pr[1]))
-
-    zero = jnp.zeros((WIDTH, 128), F32)
-    sr, si = lax.fori_loop(0, FACETS, one, (zero, zero), unroll=4)
+        mixes.append(split(jnp.concatenate([left, right], axis=1)))
+        others.append((pr[1], pi[1]))
+    sums = [dot3(split(k_ref[f]), mixes[f]) for f in range(FACETS)]
+    sr = jnp.zeros((WIDTH, 128), F32)
+    si = jnp.zeros((WIDTH, 128), F32)
+    for f in range(FACETS):
+        tr, ti = sums[f][:, :128], sums[f][:, 128:]
+        pr, pi = others[f]
+        sr = sr + (tr * pr - ti * pi)
+        si = si + (tr * pi + ti * pr)
     res = jnp.concatenate(
         [
             m_ref[0:1] - jnp.sum(sr, axis=0, keepdims=True) * (1.0 / SUBGRID),
@@ -234,16 +238,13 @@
 
 
 def image_kernel(
-    pos_ref, offset_ref, got_ref, live_ref, gamma_ref, tw_ref, b_ref, out_ref, grid, mid, trig
+    pos_ref, offset_ref, got_ref, live_ref, gamma_ref, tw_ref, b_ref, out_hbm, grid, mid, out_ref, sem
 ):
+    facet, column = pos_ref[0], pos_ref[1]
     grid[...] = jnp.zeros((3, PADDED, 128), F32)
-    for n in range(2):
-        cy, sy = half_turn(got_ref[:, 2 + n, :])
-        trig[:, 2 * n, :] = cy
-        trig[:, 2 * n + 1, :] = sy
     iota = lax.broadcasted_iota(jnp.int32, (16, 128), 0)
-    kap = (iota + 16 * pos_ref[0]).astype(F32)
-    cx, sx = live_ref[0, 0], live_ref[0, 1]
+    kap = (iota + 16 * facet).astype(F32)
+    cx, sx = live_ref[facet, 0], live_ref[facet, 1]
     one_h = jnp.where(iota == 0, 1.0, 0.0).astype(BF16)
     none_h = jnp.zeros((32, 128), BF16)
     pad = jnp.zeros((64 - WIDTH, 128), F32)
@@ -256,53 +257,62 @@
         return jnp.concatenate([hi, hit, one_h], axis=0), lo
 
     def step(g, carry):
-        c = (g * GROUP) // FACETS
-        s = (g * GROUP) % FACETS
-        gam = gamma_ref[0, c]
-        gam = jnp.concatenate([gam, gam[:, :32]], axis=1)
-        gots = [got_ref[g * GROUP + n] for n in range(GROUP)]
-        trigs = [trig[g * GROUP + n] for n in range(GROUP)]
-        us = [parts(t[0:1], t[1:2], r[2:3]) for r, t in zip(gots, trigs)]
-        gs = [dot(gam, jnp.concatenate([h, h, l], axis=0)) for h, l in us]
-        vs = [parts(t[2:3], t[3:4], r[3:4]) for r, t in zip(gots, trigs)]
-        hs = []
+        first = g * (GROUP // FACETS)
+        gots, turns = [], []
         for n in range(GROUP):
-            rr, ri = gots[n][0:1], gots[n][1:2]
-            gr, gi = gs[n][:WIDTH], gs[n][WIDTH:]
-            w = jnp.concatenate([gr * rr - gi * ri, pad, gr * ri + gi * rr, pad], axis=0)
-            wh, wl = split(w)
-            vh, vl = vs[n]
-            left = jnp.concatenate(
-                [jnp.concatenate([vh, vh], axis=1), jnp.concatenate([vl, none_h], axis=1)], axis=0
-            )
-            hs.append(dot(left, jnp.concatenate([wh, wl], axis=1), transposed=True))
-        for n in range(GROUP):
-            h = hs[n]
-            total = turn * pltpu.roll(h[WIDTH : WIDTH + 1], 64, 1)
-            o = offset_ref[c, s + n]
-            for m in range(3):
-                add = h[16 * m : 16 * m + 16]
-                if m < 2:
-                    add = add + h[64 + 16 * m : 80 + 16 * m] + total
-                at = pl.ds(o + (m + 1) % 3, 16, stride=3)
-                grid[m, at, :] = grid[m, at, :] + add
+            got = got_ref[g * GROUP + n]
+            cy, sy = half_turn(got)
+            gots.append([got[r : r + 1] for r in range(4)])
+            turns.append([(cy[r : r + 1], sy[r : r + 1]) for r in (2, 3)])
+        gs, vs, hs = {}, {}, {}
+        for b in range(0, GROUP, FACETS):
+            gam = gamma_ref[column, first + b // FACETS]
+            gam = jnp.concatenate([gam, gam[:, :32]], axis=1)
+            for n in range(b, b + FACETS):
+                h, l = parts(*turns[n][0], gots[n][2])
+                gs[n] = dot(gam, jnp.concatenate([h, h, l], axis=0))
+            for n in range(b, b + FACETS):
+                vs[n] = parts(*turns[n][1], gots[n][3])
+            for n in range(b, b + FACETS):
+                rr, ri = gots[n][0], gots[n][1]
+                gr, gi = gs[n][:WIDTH], gs[n][WIDTH:]
+                w = jnp.concatenate([gr * rr - gi * ri, pad, gr * ri + gi * rr, pad], axis=0)
+                wh, wl = split(w)
+                vh, vl = vs[n]
+                left = jnp.concatenate(
+                    [jnp.concatenate([vh, vh], axis=1), jnp.concatenate([vl, none_h], axis=1)], axis=0
+                )
+                hs[n] = dot(left, jnp.concatenate([wh, wl], axis=1), transposed=True)
+            for n in range(b, b + FACETS):
+                h = hs[n]
+                total = turn * pltpu.roll(h[WIDTH : WIDTH + 1], 64, 1)
+                o = offset_ref[first + b // FACETS, n % FACETS]
+                for m in range(3):
+                    add = h[16 * m : 16 * m + 16]
+                    if m < 2:
+                        add = add + h[64 + 16 * m : 80 + 16 * m] + total
+                    at = pl.ds(o + (m + 1) % 3, 16, stride=3)
+                    grid[m, at, :] = grid[m, at, :] + add
         return carry
 
     lax.fori_loop(0, FACETS * COLS // GROUP, step, 0)
     grid[:, 0:WIDTH, :] = grid[:, 0:WIDTH, :] + grid[:, LENGTH:PADDED, :]
     q = float(FACETS * WIDTH * WIDTH) ** (-0.25)
     right = (b_ref[0], b_ref[1])
+    lefts = []
     for beta in range(16):
         one, two, nil = (grid[m, pl.ds(beta, 128, stride=16), :] for m in range(3))
         d = (SUBGRID * q) * nil + (q * math.sqrt(3) / 4) * (one - two)
         d = (d - (0.75 * q) * turn * pltpu.roll(one + two, 64, 1)).T
-        left = split(jnp.concatenate([d[0:WIDTH], d[64 : 64 + WIDTH]], axis=1))
-        t = dot3(left, right)
-        yr, yi = t[:, :128], t[:, 128:]
+        lefts.append(split(jnp.concatenate([d[0:WIDTH], d[64 : 64 + WIDTH]], axis=1)))
+    freqs = [dot3(left, right) for left in lefts]
+    for beta in range(16):
+        yr, yi = freqs[beta][:, :128], freqs[beta][:, 128:]
         c = tw_ref[0, beta : beta + 1, :]
         s = tw_ref[1, beta : beta + 1, :]
         mid[beta, :, 0:128] = yr * c - yi * s
         mid[beta, :, 128:256] = yi * c + yr * s
+    copies = []
     for r in range(0, WIDTH, 8):
         ys = fft_list(
             [(mid[b, r : r + 8, 0:128], mid[b, r : r + 8, 128:256]) for b in range(16)], 1.0
@@ -310,6 +320,13 @@
         for t in range(16):
             out_ref[0, r : r + 8, 128 * t : 128 * t + 128] = ys[t][0]
             out_ref[1, r : r + 8, 128 * t : 128 * t + 128] = ys[t][1]
+        rows = pl.ds(r, 8)
+        copies.append(
+            pltpu.make_async_copy(out_ref.at[:, rows, :], out_hbm.at[:, rows, :], sem.at[r // 8])
+        )
+        copies[-1].start()
+    for copy in copies:
+        copy.wait()
 
 
 def keep(x):
@@ -330,9 +347,7 @@
     gamma = image_rows(a, b)
 
     def body(strips, sub_offset, uv_cells, measured):
-        facet = lax.axis_index("facet")
-        column = lax.axis_index("col")
-        pos = jnp.stack([facet, column]).astype(jnp.int32)
+        pos = jnp.stack([lax.axis_index("facet"), lax.axis_index("col")]).astype(jnp.int32)
         vm = pl.BlockSpec(memory_space=VM)
         sm = pl.BlockSpec(memory_space=SM)
         hbm = pl.BlockSpec(memory_space=pltpu.MemorySpace.HBM)
@@ -368,24 +383,15 @@
         got = lax.all_to_all(send, ("col", "facet"), split_axis=0, concat_axis=0, tiled=True)
         image = pl.pallas_call(
             image_kernel,
-            grid_spec=pltpu.PrefetchScalarGridSpec(
-                num_scalar_prefetch=2,
-                grid=(1,),
-                in_specs=[
-                    pl.BlockSpec((FACETS * COLS, 4, 128), lambda i, p, o: (0, 0, 0)),
-                    pl.BlockSpec((1, 2, 32, 128), lambda i, p, o: (p[0], 0, 0, 0)),
-                    pl.BlockSpec((1, COLS, 2 * WIDTH, 128), lambda i, p, o: (p[1], 0, 0, 0)),
-                    pl.BlockSpec((2, 16, 128), lambda i, p, o: (0, 0, 0)),
-                    pl.BlockSpec((2, 256, 256), lambda i, p, o: (0, 0, 0)),
-                ],
-                out_specs=pl.BlockSpec((2, WIDTH, LENGTH), lambda i, p, o: (0, 0, 0)),
-                scratch_shapes=[
-                    pltpu.VMEM((3, PADDED, 128), F32),
-                    pltpu.VMEM((16, WIDTH, 256), F32),
-                    pltpu.VMEM((FACETS * COLS, 4, 128), F32),
-                ],
-            ),
             out_shape=jax.ShapeDtypeStruct((2, WIDTH, LENGTH), F32),
+            in_specs=[sm, sm, vm, vm, vm, vm, vm],
+            out_specs=pl.BlockSpec(memory_space=pl.ANY),
+            scratch_shapes=[
+                pltpu.VMEM((3, PADDED, 128), F32),
+                pltpu.VMEM((16, WIDTH, 256), F32),
+                pltpu.VMEM((2, WIDTH, LENGTH), F32),
+                pltpu.SemaphoreType.DMA((6,)),
+            ],
             compiler_params=params(),
             name="image",
         )(

time: 51.7 us -> 49.4 us (0.956)
  Pallas kernels: 15.8 us -> 13.5 us
    pallas_call x1, Pallas kernels: 10.9 us -> 9.03 us  [body(): pl.pallas_call(image_kernel, out_shape=jax.ShapeDtypeStruct((2, WIDTH, LE...]
where the time goes in v3:
time: 49.4 us; the launch traced here: 49.2 us
  blocking collectives  34.8 us (70%)
  Pallas kernels  13.5 us (27%)
  between operations  0.75 us (2%)
    all_to_all x1, blocking collectives, body(): lax.all_to_all(send, ('col', 'facet'), split_axis=0, concat_axis=0, tiled...  19.1 us
    all_to_all x1, blocking collectives, body(): lax.all_to_all(windows, 'facet', split_axis=0, concat_axis=0, tiled=True)  15.7 us
    pallas_call x1, Pallas kernels, body(): pl.pallas_call(image_kernel, out_shape=jax.ShapeDtypeStruct((2, WIDTH, LE...  9.03 us
    pallas_call x1, Pallas kernels, body(): pl.pallas_call(extract_kernel, out_shape=jax.ShapeDtypeStruct((FACETS, WI...  3.12 us
    pallas_call x1, Pallas kernels, body(): pl.pallas_call(predict_kernel, out_shape=(jax.ShapeDtypeStruct((2, 128),...  1.36 us

profile of v3, /device:TPU:1, one launch (start us, length us, event | category | flops | bytes accessed | tf_op | source)
XLA Modules:
  0.0 49.2 jit_solution(16180548969470933380)
XLA Ops:
  0.6 0.0 copy-start.4
  0.6 0.0 copy-start.1
  0.7 0.0 copy-start.8
  0.7 0.0 copy-start.7
  0.7 0.1 pad_add_fusion.col_ref.pos_ref
  0.8 3.1 %extract.1 = f32[16,48,128]{2,1,0:T(8,128)S(1)} custom-call(s32[2]{0:T(128)S(1)} %pad_add_fusion.col_ref.pos_ref, s32[8,16]{1,0:T(8,128)} %offset_ref.1, f32[2,48,2048]{2,1,0:T(8,128)} %bitcast.9, f32[2,16,128]{2,1,0:T(8,128)} %constant.23.clone.tw_hbm.tw_ref, bf16[2,128,256]{2,1,0:T(8,128)(2,1)} %constant.24.clone.f_hbm), custom_call_target="tpu_custom_call" | custom-call | tf_op jit(solution)/shard_map/extract/pallas_call | solution.py:354
  3.9 0.0 copy-start
  3.9 0.0 copy-start.2
  3.9 0.0 copy-start.3
  3.9 0.0 copy-start.5
  3.9 0.0 copy-start.6
  3.9 15.7 %all_to_all.10.k_ref = f32[16,48,128]{2,1,0:T(8,128)S(1)} all-to-all(f32[16,48,128]{2,1,0:T(8,128)S(1)} %extract.1), channel_id=1, replica_groups=mesh['facet'=16,'col'=8] {'facet'}, dimensions={0} | all-to-all | bytes 786432 | tf_op jit(solution)/shard_map/all_to_all | solution.py:371
  19.6 0.0 copy-done.4
  19.6 0.0 copy-done.1
  19.6 0.0 copy-done.8
  19.6 0.0 copy-done.7
  19.6 1.4 %predict.1 = (f32[2,128]{1,0:T(2,128)}, f32[128,4,128]{2,1,0:T(4,128)S(1)}) custom-call(f32[16,48,128]{2,1,0:T(8,128)S(1)} %all_to_all.10.k_ref, s32[2,128]{1,0:T(2,128)S(1)} %bitcast.7, f32[2,128]{1,0:T(2,128)S(1)} %bitcast.8, f32[16,2,48,128]{3,2,1,0:T(8,128)S(1)} %copy-done.1, f32[4,48,128]{2,1,0:T(8,128)S(1)} %copy-done.4), custom_call_target="tpu_custom_call" | custom-call | tf_op jit(solution)/shard_map/predict/pallas_call | solution.py:372
  21.0 19.1 %all_to_all.11.got_ref = f32[128,4,128]{2,1,0:T(4,128)S(1)} all-to-all(f32[128,4,128]{2,1,0:T(4,128)S(1)} %get-tuple-element.4), channel_id=1, replica_groups=mesh['facet'=16,'col'=8] {'col','facet'}, dimensions={0} | all-to-all | bytes 524288 | tf_op jit(solution)/shard_map/all_to_all | solution.py:383
  40.1 0.0 copy-done
  40.1 0.0 copy-done.2
  40.1 0.0 copy-done.3
  40.1 0.0 copy-done.5
  40.1 0.0 copy-done.6
  40.2 9.0 %image.1 = f32[2,48,2048]{2,1,0:T(8,128)} custom-call(s32[2]{0:T(128)S(1)} %pad_add_fusion.col_ref.pos_ref, s32[8,16]{1,0:T(8,128)S(1)} %copy-done.6, f32[128,4,128]{2,1,0:T(4,128)S(1)} %all_to_all.11.got_ref, f32[16,2,32,128]{3,2,1,0:T(8,128)S(1)} %copy-done.2, bf16[8,8,96,128]{3,2,1,0:T(8,128)(2,1)S(1)} %copy-done, f32[2,16,128]{2,1,0:T(8,128)S(1)} %copy-done.5, ...), custom_call_target="tpu_custom_call" | custom-call | tf_op jit(solution)/shard_map/image/pallas_call | solution.py:384
Async XLA Ops:
  0.6 19.0 %copy-start.4 = (f32[4,48,128]{2,1,0:T(8,128)S(1)}, f32[4,48,128]{2,1,0:T(8,128)}, u32[]{:S(2)}) copy-start(f32[4,48,128]{2,1,0:T(8,128)} %constant.26.clone.coef_ref) | copy-start | bytes 294916
  0.6 19.0 %copy-start.1 = (f32[16,2,48,128]{3,2,1,0:T(8,128)S(1)}, f32[16,2,48,128]{3,2,1,0:T(8,128)}, u32[]{:S(2)}) copy-start(f32[16,2,48,128]{3,2,1,0:T(8,128)} %constant.25.clone.rows_ref) | copy-start | bytes 2359300
  0.7 19.0 %copy-start.8 = (f32[1,1,2,128]{3,2,1,0:T(2,128)S(1)}, f32[1,1,2,128]{3,2,1,0:T(2,128)}, u32[]{:S(2)}) copy-start(f32[1,1,2,128]{3,2,1,0:T(2,128)} %param.14) | copy-start | bytes 3076
  0.7 19.0 %copy-start.7 = (s32[1,1,2,128]{3,2,1,0:T(2,128)S(1)}, s32[1,1,2,128]{3,2,1,0:T(2,128)}, u32[]{:S(2)}) copy-start(s32[1,1,2,128]{3,2,1,0:T(2,128)} %param.13) | copy-start | bytes 3076
  3.9 36.2 %copy-start = (bf16[8,8,96,128]{3,2,1,0:T(8,128)(2,1)S(1)}, bf16[8,8,96,128]{3,2,1,0:T(8,128)(2,1)}, u32[]{:S(2)}) copy-start(bf16[8,8,96,128]{3,2,1,0:T(8,128)(2,1)} %constant.28.clone.gamma_ref) | copy-start | bytes 4718596
  3.9 36.2 %copy-start.2 = (f32[16,2,32,128]{3,2,1,0:T(8,128)S(1)}, f32[16,2,32,128]{3,2,1,0:T(8,128)}, u32[]{:S(2)}) copy-start(f32[16,2,32,128]{3,2,1,0:T(8,128)} %constant.27.clone.live_ref) | copy-start | bytes 1572868
  3.9 36.2 %copy-start.3 = (bf16[2,256,256]{2,1,0:T(8,128)(2,1)S(1)}, bf16[2,256,256]{2,1,0:T(8,128)(2,1)}, u32[]{:S(2)}) copy-start(bf16[2,256,256]{2,1,0:T(8,128)(2,1)} %constant.29.clone.b_ref) | copy-start | bytes 786436
  3.9 36.2 %copy-start.5 = (f32[2,16,128]{2,1,0:T(8,128)S(1)}, f32[2,16,128]{2,1,0:T(8,128)}, u32[]{:S(2)}) copy-start(f32[2,16,128]{2,1,0:T(8,128)} %constant.23.clone.tw_hbm.tw_ref) | copy-start | bytes 49156
  3.9 36.2 %copy-start.6 = (s32[8,16]{1,0:T(8,128)S(1)}, s32[8,16]{1,0:T(8,128)}, u32[]{:S(2)}) copy-start(s32[8,16]{1,0:T(8,128)} %offset_ref.1) | copy-start | bytes 1540

commit v4 on v3

--- a/solution.py
+++ b/solution.py
@@ -14,7 +14,9 @@
 LENGTH = 2048
 FACETS = 16
 COLS = 8
-GROUP = 32
+GROUP = 128
+LAG1 = 8
+LAG2 = 16
 ROWS = 384
 PADDED = LENGTH + WIDTH
 TOTAL = FACETS * WIDTH
@@ -43,7 +45,9 @@
 
 def dot3(a, b, transposed=False):
     (ah, al), (bh, bl) = a, b
-    return dot(ah, bh, transposed) + dot(ah, bl, transposed) + dot(al, bh, transposed)
+    rows = ah.shape[0]
+    both = dot(jnp.concatenate([ah, al], axis=0), bh, transposed)
+    return both[:rows] + both[rows:] + dot(ah, bl, transposed)
 
 
 def fft_list(xs, sign):
@@ -93,8 +97,9 @@
     )
     kappa = np.arange(TOTAL).reshape(FACETS, WIDTH, 1) * np.ones((1, 1, 128))
     angle = np.pi * kappa / TOTAL
-    rows = np.stack([np.cos(angle), np.sin(angle)], axis=1).astype(np.float32)
-    live = np.ascontiguousarray(rows[:, :, ORDER[:32]])
+    cot = np.where(kappa % 3 == 0, 0.0, 1 / np.tan(np.where(kappa % 3 == 0, 1.0, angle)))
+    rows = cot.astype(np.float32)
+    live = np.ascontiguousarray(rows[:, ORDER[:32]])
     q = float(FACETS * WIDTH * WIDTH) ** (-0.25)
     k = np.arange(WIDTH)
     numer = np.exp(2j * np.pi * (k % 3) / 3) - 1
@@ -135,19 +140,19 @@
     c = 1.0 / math.factorial(12)
     for n in (10, 8, 6, 4, 2, 0):
         c = c * w + (1.0 if n % 4 == 0 else -1.0) / math.factorial(n)
-    return -(s * z), c
-
-
-def ratio(cx, sx, cy, sy):
-    return (cx * cy + sx * sy) / (sx * cy - cx * sy)
-
-
-def cotangent(cx, sx, cy, sy, kappa, cell3, threes):
-    return jnp.where(threes, jnp.where(kappa == cell3, 1.0, 0.0), ratio(cx, sx, cy, sy))
+    return jnp.where(cell == 0.0, 1e30, -(s * z) / c)
+
+
+def ratio(cot, square, turn):
+    return cot + square / (turn - cot)
+
+
+def cotangent(cot, square, turn, kappa, cell3, threes):
+    return jnp.where(threes, jnp.where(kappa == cell3, 1.0, 0.0), ratio(cot, square, turn))
 
 
 def extract_kernel(
-    col_ref, offset_hbm, x_hbm, tw_hbm, f_hbm, out_ref, mid, spectrum, offset_ref, x_ref, tw_ref, f_ref, sem
+    offset_hbm, x_hbm, tw_hbm, f_hbm, out_ref, mid, spectrum, offset_ref, x_ref, tw_ref, f_ref, sem
 ):
     copies = [pltpu.make_async_copy(tw_hbm, tw_ref, sem.at[6])]
     for n in range(6):
@@ -189,14 +194,14 @@
         half = 128 * (beta % 2)
         spectrum[pl.ds(beta, 128, stride=16), :] = freqs[beta // 2][:, half : half + 128]
     spectrum[LENGTH:PADDED, :] = spectrum[0:WIDTH, :]
-    column = col_ref[1]
+    column = lax.axis_index("col")
     for s in range(FACETS):
         out_ref[s] = spectrum[pl.ds(offset_ref[column, s], WIDTH), :]
 
 
 def predict_kernel(k_ref, uv_ref, m_ref, rows_ref, coef_ref, res_ref, send_ref):
     uv = uv_ref[...].astype(F32)
-    cy, sy = half_turn(uv)
+    angles = half_turn(uv)
     iota = lax.broadcasted_iota(jnp.int32, (WIDTH, 128), 0)
     threes = iota % 3 == 0
     kap = iota.astype(F32)
@@ -205,13 +210,14 @@
 
     mixes, others = [], []
     for f in range(FACETS):
-        cx, sx = rows_ref[f, 0], rows_ref[f, 1]
+        cot = rows_ref[f]
+        square = 1.0 + cot * cot
         pr, pi = [], []
         for n in range(2):
             cell = 3.0 * uv[n : n + 1] - float(f * WIDTH)
-            cot = cotangent(cx, sx, cy[n : n + 1], sy[n : n + 1], kap, cell, threes)
-            pr.append(ar + br * cot)
-            pi.append(ai + bi * cot)
+            value = cotangent(cot, square, angles[n : n + 1], kap, cell, threes)
+            pr.append(ar + br * value)
+            pi.append(ai + bi * value)
         left = jnp.concatenate([pr[0], zeros, -pi[0], zeros], axis=0)
         right = jnp.concatenate([pi[0], zeros, pr[0], zeros], axis=0)
         mixes.append(split(jnp.concatenate([left, right], axis=1)))
@@ -238,61 +244,74 @@
 
 
 def image_kernel(
-    pos_ref, offset_ref, got_ref, live_ref, gamma_ref, tw_ref, b_ref, out_hbm, grid, mid, out_ref, sem
+    offset_hbm, got_ref, live_ref, gamma_ref, tw_ref, b_ref, out_hbm, grid, mid, out_ref, offset_ref, sem
 ):
-    facet, column = pos_ref[0], pos_ref[1]
+    fetch = pltpu.make_async_copy(offset_hbm, offset_ref, sem.at[6])
+    fetch.start()
+    facet, column = lax.axis_index("facet"), lax.axis_index("col")
     grid[...] = jnp.zeros((3, PADDED, 128), F32)
     iota = lax.broadcasted_iota(jnp.int32, (16, 128), 0)
     kap = (iota + 16 * facet).astype(F32)
-    cx, sx = live_ref[facet, 0], live_ref[facet, 1]
+    cot = live_ref[facet]
+    square = 1.0 + cot * cot
     one_h = jnp.where(iota == 0, 1.0, 0.0).astype(BF16)
     none_h = jnp.zeros((32, 128), BF16)
     pad = jnp.zeros((64 - WIDTH, 128), F32)
     lanes = lax.broadcasted_iota(jnp.int32, (1, 128), 1)
     turn = jnp.where(lanes < 64, -1.0, 1.0)
 
-    def parts(cy, sy, cell):
-        hi, lo = split(ratio(cx, sx, cy, sy))
+    def parts(angle, cell):
+        hi, lo = split(ratio(cot, square, angle))
         hit = jnp.where(kap == cell, 1.0, 0.0).astype(BF16)
         return jnp.concatenate([hi, hit, one_h], axis=0), lo
+
+    fetch.wait()
 
     def step(g, carry):
         first = g * (GROUP // FACETS)
         gots, turns = [], []
         for n in range(GROUP):
             got = got_ref[g * GROUP + n]
-            cy, sy = half_turn(got)
+            angles = half_turn(got)
             gots.append([got[r : r + 1] for r in range(4)])
-            turns.append([(cy[r : r + 1], sy[r : r + 1]) for r in (2, 3)])
+            turns.append([angles[r : r + 1] for r in (2, 3)])
         gs, vs, hs = {}, {}, {}
-        for b in range(0, GROUP, FACETS):
-            gam = gamma_ref[column, first + b // FACETS]
-            gam = jnp.concatenate([gam, gam[:, :32]], axis=1)
-            for n in range(b, b + FACETS):
-                h, l = parts(*turns[n][0], gots[n][2])
-                gs[n] = dot(gam, jnp.concatenate([h, h, l], axis=0))
-            for n in range(b, b + FACETS):
-                vs[n] = parts(*turns[n][1], gots[n][3])
-            for n in range(b, b + FACETS):
-                rr, ri = gots[n][0], gots[n][1]
-                gr, gi = gs[n][:WIDTH], gs[n][WIDTH:]
-                w = jnp.concatenate([gr * rr - gi * ri, pad, gr * ri + gi * rr, pad], axis=0)
-                wh, wl = split(w)
-                vh, vl = vs[n]
-                left = jnp.concatenate(
-                    [jnp.concatenate([vh, vh], axis=1), jnp.concatenate([vl, none_h], axis=1)], axis=0
-                )
-                hs[n] = dot(left, jnp.concatenate([wh, wl], axis=1), transposed=True)
-            for n in range(b, b + FACETS):
-                h = hs[n]
-                total = turn * pltpu.roll(h[WIDTH : WIDTH + 1], 64, 1)
-                o = offset_ref[first + b // FACETS, n % FACETS]
-                for m in range(3):
-                    add = h[16 * m : 16 * m + 16]
-                    if m < 2:
-                        add = add + h[64 + 16 * m : 80 + 16 * m] + total
-                    at = pl.ds(o + (m + 1) % 3, 16, stride=3)
-                    grid[m, at, :] = grid[m, at, :] + add
+
+        def gamma(n):
+            gam = gamma_ref[column, first + n // FACETS]
+            return jnp.concatenate([gam, gam[:, :32]], axis=1)
+
+        def rows_of(n):
+            h, l = parts(turns[n][0], gots[n][2])
+            gs[n] = dot(gamma(n), jnp.concatenate([h, h, l], axis=0))
+            vs[n] = parts(turns[n][1], gots[n][3])
+
+        def columns_of(n):
+            rr, ri = gots[n][0], gots[n][1]
+            gr, gi = gs[n][:WIDTH], gs[n][WIDTH:]
+            w = jnp.concatenate([gr * rr - gi * ri, pad, gr * ri + gi * rr, pad], axis=0)
+            wh, wl = split(w)
+            vh, vl = vs[n]
+            left = jnp.concatenate(
+                [jnp.concatenate([vh, vh], axis=1), jnp.concatenate([vl, none_h], axis=1)], axis=0
+            )
+            hs[n] = dot(left, jnp.concatenate([wh, wl], axis=1), transposed=True)
+
+        def place(n):
+            h = hs[n]
+            total = turn * pltpu.roll(h[WIDTH : WIDTH + 1], 64, 1)
+            o = offset_ref[first + n // FACETS, n % FACETS]
+            for m in range(3):
+                add = h[16 * m : 16 * m + 16]
+                if m < 2:
+                    add = add + h[64 + 16 * m : 80 + 16 * m] + total
+                at = pl.ds(o + (m + 1) % 3, 16, stride=3)
+                grid[m, at, :] = grid[m, at, :] + add
+
+        for n in range(GROUP + LAG2):
+            for fn, lag in ((rows_of, 0), (columns_of, LAG1), (place, LAG2)):
+                if 0 <= n - lag < GROUP:
+                    fn(n - lag)
         return carry
 
     lax.fori_loop(0, FACETS * COLS // GROUP, step, 0)
@@ -338,7 +357,6 @@
 
 
 VM = pltpu.MemorySpace.VMEM
-SM = pltpu.MemorySpace.SMEM
 
 
 def solution(mesh):
@@ -347,14 +365,12 @@
     gamma = image_rows(a, b)
 
     def body(strips, sub_offset, uv_cells, measured):
-        pos = jnp.stack([lax.axis_index("facet"), lax.axis_index("col")]).astype(jnp.int32)
         vm = pl.BlockSpec(memory_space=VM)
-        sm = pl.BlockSpec(memory_space=SM)
         hbm = pl.BlockSpec(memory_space=pltpu.MemorySpace.HBM)
         windows = pl.pallas_call(
             extract_kernel,
             out_shape=jax.ShapeDtypeStruct((FACETS, WIDTH, 128), F32),
-            in_specs=[sm, hbm, hbm, hbm, hbm],
+            in_specs=[hbm, hbm, hbm, hbm],
             out_specs=vm,
             scratch_shapes=[
                 pltpu.VMEM((16, 64, 256), F32),
@@ -367,7 +383,7 @@
             ],
             compiler_params=params(),
             name="extract",
-        )(pos, *(keep(x) for x in (sub_offset, strips[0], jnp.asarray(twiddle), jnp.asarray(forward))))
+        )(*(keep(x) for x in (sub_offset, strips[0], jnp.asarray(twiddle), jnp.asarray(forward))))
         arrived = lax.all_to_all(windows, "facet", split_axis=0, concat_axis=0, tiled=True)
         res, send = pl.pallas_call(
             predict_kernel,
@@ -384,19 +400,19 @@
         image = pl.pallas_call(
             image_kernel,
             out_shape=jax.ShapeDtypeStruct((2, WIDTH, LENGTH), F32),
-            in_specs=[sm, sm, vm, vm, vm, vm, vm],
+            in_specs=[hbm, vm, vm, vm, vm, vm],
             out_specs=pl.BlockSpec(memory_space=pl.ANY),
             scratch_shapes=[
                 pltpu.VMEM((3, PADDED, 128), F32),
                 pltpu.VMEM((16, WIDTH, 256), F32),
                 pltpu.VMEM((2, WIDTH, LENGTH), F32),
-                pltpu.SemaphoreType.DMA((6,)),
+                pltpu.SMEM((COLS, FACETS), jnp.int32),
+                pltpu.SemaphoreType.DMA((7,)),
             ],
             compiler_params=params(),
             name="image",
         )(
-            pos,
-            sub_offset,
+            keep(sub_offset),
             got,
             jnp.asarray(live),
             jnp.asarray(gamma),

time: 49.4 us -> 47.1 us (0.953)
  Pallas kernels: 13.5 us -> 11.5 us
    pallas_call x1, Pallas kernels: 9.03 us -> 7.67 us  [body(): pl.pallas_call(image_kernel, out_shape=jax.ShapeDtypeStruct((2, WIDTH, LE...]
    pallas_call x1, Pallas kernels: 3.12 us -> 2.42 us  [body(): pl.pallas_call(extract_kernel, out_shape=jax.ShapeDtypeStruct((FACETS, WI...]
where the time goes in v4:
time: 47.1 us; the launch traced here: 46.9 us
  blocking collectives  34.7 us (74%)
  Pallas kernels  11.5 us (24%)
  between operations  0.73 us (2%)
    all_to_all x1, blocking collectives, body(): lax.all_to_all(send, ('col', 'facet'), split_axis=0, concat_axis=0, tiled...  19.1 us
    all_to_all x1, blocking collectives, body(): lax.all_to_all(windows, 'facet', split_axis=0, concat_axis=0, tiled=True)  15.5 us
    pallas_call x1, Pallas kernels, body(): pl.pallas_call(image_kernel, out_shape=jax.ShapeDtypeStruct((2, WIDTH, LE...  7.67 us
    pallas_call x1, Pallas kernels, body(): pl.pallas_call(extract_kernel, out_shape=jax.ShapeDtypeStruct((FACETS, WI...  2.42 us
    pallas_call x1, Pallas kernels, body(): pl.pallas_call(predict_kernel, out_shape=(jax.ShapeDtypeStruct((2, 128),...  1.36 us

profile of v4, /device:TPU:1, one launch (start us, length us, event | category | flops | bytes accessed | tf_op | source)
XLA Modules:
  0.0 46.9 jit_solution(17901318360909574805)
XLA Ops:
  0.6 0.0 copy-start.4
  0.6 0.0 copy-start.1
  0.7 0.0 copy-start.7
  0.7 0.0 copy-start.6
  0.7 0.0 copy-start
  0.7 0.0 copy-start.2
  0.7 0.0 copy-start.3
  0.7 0.0 copy-start.5
  0.7 2.4 %extract.1 = f32[16,48,128]{2,1,0:T(8,128)S(1)} custom-call(s32[8,16]{1,0:T(8,128)} %offset_hbm.3, f32[2,48,2048]{2,1,0:T(8,128)} %bitcast.7, f32[2,16,128]{2,1,0:T(8,128)} %constant.14.clone.tw_hbm.tw_ref, bf16[2,128,256]{2,1,0:T(8,128)(2,1)} %constant.15.clone.f_hbm), custom_call_target="tpu_custom_call" | custom-call | tf_op jit(solution)/shard_map/extract/pallas_call | solution.py:370
  3.2 15.5 %all_to_all.10.k_ref = f32[16,48,128]{2,1,0:T(8,128)S(1)} all-to-all(f32[16,48,128]{2,1,0:T(8,128)S(1)} %extract.1), channel_id=1, replica_groups=mesh['facet'=16,'col'=8] {'facet'}, dimensions={0} | all-to-all | bytes 786432 | tf_op jit(solution)/shard_map/all_to_all | solution.py:387
  18.7 0.0 copy-done.4
  18.7 0.0 copy-done.1
  18.7 0.0 copy-done.7
  18.7 0.0 copy-done.6
  18.7 1.4 %predict.1 = (f32[2,128]{1,0:T(2,128)}, f32[128,4,128]{2,1,0:T(4,128)S(1)}) custom-call(f32[16,48,128]{2,1,0:T(8,128)S(1)} %all_to_all.10.k_ref, s32[2,128]{1,0:T(2,128)S(1)} %bitcast.5, f32[2,128]{1,0:T(2,128)S(1)} %bitcast.6, f32[16,48,128]{2,1,0:T(8,128)S(1)} %copy-done.1, f32[4,48,128]{2,1,0:T(8,128)S(1)} %copy-done.4), custom_call_target="tpu_custom_call" | custom-call | tf_op jit(solution)/shard_map/predict/pallas_call | solution.py:388
  20.1 19.1 %all_to_all.11.got_ref = f32[128,4,128]{2,1,0:T(4,128)S(1)} all-to-all(f32[128,4,128]{2,1,0:T(4,128)S(1)} %get-tuple-element.4), channel_id=1, replica_groups=mesh['facet'=16,'col'=8] {'col','facet'}, dimensions={0} | all-to-all | bytes 524288 | tf_op jit(solution)/shard_map/all_to_all | solution.py:399
  39.2 0.0 copy-done
  39.2 0.0 copy-done.2
  39.2 0.0 copy-done.3
  39.2 0.0 copy-done.5
  39.2 7.7 %image.1 = f32[2,48,2048]{2,1,0:T(8,128)} custom-call(s32[8,16]{1,0:T(8,128)} %offset_hbm.3, f32[128,4,128]{2,1,0:T(4,128)S(1)} %all_to_all.11.got_ref, f32[16,32,128]{2,1,0:T(8,128)S(1)} %copy-done.3, bf16[8,8,96,128]{3,2,1,0:T(8,128)(2,1)S(1)} %copy-done, f32[2,16,128]{2,1,0:T(8,128)S(1)} %copy-done.5, bf16[2,256,256]{2,1,0:T(8,128)(2,1)S(1)} %copy-done.2), custom_call_target="tpu_custom_call" | custom-call | tf_op jit(solution)/shard_map/image/pallas_call | solution.py:400
Async XLA Ops:
  0.6 18.1 %copy-start.4 = (f32[4,48,128]{2,1,0:T(8,128)S(1)}, f32[4,48,128]{2,1,0:T(8,128)}, u32[]{:S(2)}) copy-start(f32[4,48,128]{2,1,0:T(8,128)} %constant.17.clone.coef_ref) | copy-start | bytes 294916
  0.6 18.1 %copy-start.1 = (f32[16,48,128]{2,1,0:T(8,128)S(1)}, f32[16,48,128]{2,1,0:T(8,128)}, u32[]{:S(2)}) copy-start(f32[16,48,128]{2,1,0:T(8,128)} %constant.16.clone.rows_ref) | copy-start | bytes 1179652
  0.7 18.1 %copy-start.7 = (f32[1,1,2,128]{3,2,1,0:T(2,128)S(1)}, f32[1,1,2,128]{3,2,1,0:T(2,128)}, u32[]{:S(2)}) copy-start(f32[1,1,2,128]{3,2,1,0:T(2,128)} %param.14) | copy-start | bytes 3076
  0.7 18.1 %copy-start.6 = (s32[1,1,2,128]{3,2,1,0:T(2,128)S(1)}, s32[1,1,2,128]{3,2,1,0:T(2,128)}, u32[]{:S(2)}) copy-start(s32[1,1,2,128]{3,2,1,0:T(2,128)} %param.13) | copy-start | bytes 3076
  0.7 38.5 %copy-start = (bf16[8,8,96,128]{3,2,1,0:T(8,128)(2,1)S(1)}, bf16[8,8,96,128]{3,2,1,0:T(8,128)(2,1)}, u32[]{:S(2)}) copy-start(bf16[8,8,96,128]{3,2,1,0:T(8,128)(2,1)} %constant.19.clone.gamma_ref) | copy-start | bytes 4718596
  0.7 38.5 %copy-start.2 = (bf16[2,256,256]{2,1,0:T(8,128)(2,1)S(1)}, bf16[2,256,256]{2,1,0:T(8,128)(2,1)}, u32[]{:S(2)}) copy-start(bf16[2,256,256]{2,1,0:T(8,128)(2,1)} %constant.20.clone.b_ref) | copy-start | bytes 786436
  0.7 38.5 %copy-start.3 = (f32[16,32,128]{2,1,0:T(8,128)S(1)}, f32[16,32,128]{2,1,0:T(8,128)}, u32[]{:S(2)}) copy-start(f32[16,32,128]{2,1,0:T(8,128)} %constant.18.clone.live_ref) | copy-start | bytes 786436
  0.7 38.5 %copy-start.5 = (f32[2,16,128]{2,1,0:T(8,128)S(1)}, f32[2,16,128]{2,1,0:T(8,128)}, u32[]{:S(2)}) copy-start(f32[2,16,128]{2,1,0:T(8,128)} %constant.14.clone.tw_hbm.tw_ref) | copy-start | bytes 49156

commit v5 on v4

--- a/solution.py
+++ b/solution.py
@@ -11,6 +11,7 @@
 
 SUBGRID = 256
 WIDTH = 48
+SENT = 40
 LENGTH = 2048
 FACETS = 16
 COLS = 8
@@ -162,7 +163,6 @@
     copies.append(pltpu.make_async_copy(offset_hbm, offset_ref, sem.at[8]))
     for copy in copies:
         copy.start()
-    mid[:, WIDTH:64, :] = jnp.zeros((16, 64 - WIDTH, 256), F32)
     copies[0].wait()
     for r in range(0, WIDTH, 8):
         copies[1 + r // 8].wait()
@@ -180,14 +180,15 @@
     copies[7].wait()
     copies[8].wait()
     left = (f_ref[0], f_ref[1])
+    none = jnp.zeros((128 - 2 * WIDTH, 256), BF16)
     rights = []
     for beta in range(0, 16, 2):
         his, los = [], []
         for b in (beta, beta + 1):
             rh, rl = split(mid[b, :, 0:128])
             ih, il = split(mid[b, :, 128:256])
-            his += [jnp.concatenate([rh, ih], axis=1), jnp.concatenate([ih, -rh], axis=1)]
-            los += [jnp.concatenate([rl, il], axis=1), jnp.concatenate([il, -rl], axis=1)]
+            his += [jnp.concatenate([rh, ih], axis=1), jnp.concatenate([ih, -rh], axis=1), none]
+            los += [jnp.concatenate([rl, il], axis=1), jnp.concatenate([il, -rl], axis=1), none]
         rights.append((jnp.concatenate(his, axis=0), jnp.concatenate(los, axis=0)))
     freqs = [dot3(left, right, transposed=True) for right in rights]
     for beta in range(16):
@@ -195,8 +196,15 @@
         spectrum[pl.ds(beta, 128, stride=16), :] = freqs[beta // 2][:, half : half + 128]
     spectrum[LENGTH:PADDED, :] = spectrum[0:WIDTH, :]
     column = lax.axis_index("col")
+    free = lax.broadcasted_iota(jnp.int32, (8, 128), 1) >= 96
     for s in range(FACETS):
-        out_ref[s] = spectrum[pl.ds(offset_ref[column, s], WIDTH), :]
+        o = offset_ref[column, s]
+        tail = spectrum[pl.ds(o + SENT, WIDTH - SENT), :]
+        for n in range(SENT // 8):
+            rows = spectrum[pl.ds(o + 8 * n, 8), :]
+            if n < 3:
+                rows = jnp.where(free, pltpu.roll(tail, 96 - 32 * n, 1), rows)
+            out_ref[s, 8 * n : 8 * n + 8, :] = rows
 
 
 def predict_kernel(k_ref, uv_ref, m_ref, rows_ref, coef_ref, res_ref, send_ref):
@@ -206,7 +214,16 @@
     threes = iota % 3 == 0
     kap = iota.astype(F32)
     ar, ai, br, bi = (coef_ref[n] for n in range(4))
-    zeros = jnp.zeros((16, 128), F32)
+    zeros = jnp.zeros((128 - 2 * WIDTH, 128), F32)
+    lane = lax.broadcasted_iota(jnp.int32, (8, 128), 1)
+
+    def unpack(f):
+        tail = pltpu.roll(k_ref[f, 0:8, :], 32, 1)
+        for n in (1, 2):
+            piece = pltpu.roll(k_ref[f, 8 * n : 8 * n + 8, :], 32 * n + 32, 1)
+            tail = jnp.where(lane < 32 * n, tail, piece)
+        return split(jnp.concatenate([k_ref[f], tail], axis=0))
+
 
     mixes, others = [], []
     for f in range(FACETS):
@@ -218,11 +235,11 @@
             value = cotangent(cot, square, angles[n : n + 1], kap, cell, threes)
             pr.append(ar + br * value)
             pi.append(ai + bi * value)
-        left = jnp.concatenate([pr[0], zeros, -pi[0], zeros], axis=0)
-        right = jnp.concatenate([pi[0], zeros, pr[0], zeros], axis=0)
+        left = jnp.concatenate([pr[0], -pi[0], zeros], axis=0)
+        right = jnp.concatenate([pi[0], pr[0], zeros], axis=0)
         mixes.append(split(jnp.concatenate([left, right], axis=1)))
         others.append((pr[1], pi[1]))
-    sums = [dot3(split(k_ref[f]), mixes[f]) for f in range(FACETS)]
+    sums = [dot3(unpack(f), mixes[f]) for f in range(FACETS)]
     sr = jnp.zeros((WIDTH, 128), F32)
     si = jnp.zeros((WIDTH, 128), F32)
     for f in range(FACETS):
@@ -317,12 +334,14 @@
     lax.fori_loop(0, FACETS * COLS // GROUP, step, 0)
     grid[:, 0:WIDTH, :] = grid[:, 0:WIDTH, :] + grid[:, LENGTH:PADDED, :]
     q = float(FACETS * WIDTH * WIDTH) ** (-0.25)
+    for row in range(0, LENGTH, 64):
+        one, two, nil = (grid[m, row : row + 64, :] for m in range(3))
+        d = (SUBGRID * q) * nil + (q * math.sqrt(3) / 4) * (one - two)
+        grid[2, row : row + 64, :] = d - (0.75 * q) * turn * pltpu.roll(one + two, 64, 1)
     right = (b_ref[0], b_ref[1])
     lefts = []
     for beta in range(16):
-        one, two, nil = (grid[m, pl.ds(beta, 128, stride=16), :] for m in range(3))
-        d = (SUBGRID * q) * nil + (q * math.sqrt(3) / 4) * (one - two)
-        d = (d - (0.75 * q) * turn * pltpu.roll(one + two, 64, 1)).T
+        d = grid[2, pl.ds(beta, 128, stride=16), :].T
         lefts.append(split(jnp.concatenate([d[0:WIDTH], d[64 : 64 + WIDTH]], axis=1)))
     freqs = [dot3(left, right) for left in lefts]
     for beta in range(16):
@@ -369,11 +388,11 @@
         hbm = pl.BlockSpec(memory_space=pltpu.MemorySpace.HBM)
         windows = pl.pallas_call(
             extract_kernel,
-            out_shape=jax.ShapeDtypeStruct((FACETS, WIDTH, 128), F32),
+            out_shape=jax.ShapeDtypeStruct((FACETS, SENT, 128), F32),
             in_specs=[hbm, hbm, hbm, hbm],
             out_specs=vm,
             scratch_shapes=[
-                pltpu.VMEM((16, 64, 256), F32),
+                pltpu.VMEM((16, WIDTH, 256), F32),
                 pltpu.VMEM((PADDED, 128), F32),
                 pltpu.SMEM((COLS, FACETS), jnp.int32),
                 pltpu.VMEM((2, WIDTH, LENGTH), F32),

time: 47.1 us -> 46 us (0.977)
  blocking collectives: 34.7 us -> 34 us
  Pallas kernels: 11.5 us -> 11 us
    all_to_all x1, blocking collectives: 15.5 us -> 15 us  [body(): lax.all_to_all(windows, 'facet', split_axis=0, concat_axis=0, tiled=True)]
    pallas_call x1, Pallas kernels: 7.67 us -> 7.19 us  [body(): pl.pallas_call(image_kernel, out_shape=jax.ShapeDtypeStruct((2, WIDTH, LE...]
where the time goes in v5:
time: 46 us; the launch traced here: 45.8 us
  blocking collectives  34 us (74%)
  Pallas kernels  11 us (24%)
  between operations  0.73 us (2%)
    all_to_all x1, blocking collectives, body(): lax.all_to_all(send, ('col', 'facet'), split_axis=0, concat_axis=0, tiled...  19 us
    all_to_all x1, blocking collectives, body(): lax.all_to_all(windows, 'facet', split_axis=0, concat_axis=0, tiled=True)  15 us
    pallas_call x1, Pallas kernels, body(): pl.pallas_call(image_kernel, out_shape=jax.ShapeDtypeStruct((2, WIDTH, LE...  7.19 us
    pallas_call x1, Pallas kernels, body(): pl.pallas_call(extract_kernel, out_shape=jax.ShapeDtypeStruct((FACETS, SE...  2.48 us
    pallas_call x1, Pallas kernels, body(): pl.pallas_call(predict_kernel, out_shape=(jax.ShapeDtypeStruct((2, 128),...  1.35 us

profile of v5, /device:TPU:1, one launch (start us, length us, event | category | flops | bytes accessed | tf_op | source)
XLA Modules:
  0.0 45.8 jit_solution(5370517550171171099)
XLA Ops:
  0.6 0.0 copy-start.4
  0.6 0.0 copy-start.1
  0.7 0.0 copy-start.7
  0.7 0.0 copy-start.6
  0.7 0.0 copy-start
  0.7 0.0 copy-start.2
  0.7 0.0 copy-start.3
  0.7 0.0 copy-start.5
  0.7 2.5 %extract.1 = f32[16,40,128]{2,1,0:T(8,128)S(1)} custom-call(s32[8,16]{1,0:T(8,128)} %offset_hbm.3, f32[2,48,2048]{2,1,0:T(8,128)} %bitcast.7, f32[2,16,128]{2,1,0:T(8,128)} %constant.14.clone.tw_hbm.tw_ref, bf16[2,128,256]{2,1,0:T(8,128)(2,1)} %constant.15.clone.f_hbm), custom_call_target="tpu_custom_call" | custom-call | tf_op jit(solution)/shard_map/extract/pallas_call | solution.py:389
  3.2 15.0 %all_to_all.10.k_ref = f32[16,40,128]{2,1,0:T(8,128)S(1)} all-to-all(f32[16,40,128]{2,1,0:T(8,128)S(1)} %extract.1), channel_id=1, replica_groups=mesh['facet'=16,'col'=8] {'facet'}, dimensions={0} | all-to-all | bytes 655360 | tf_op jit(solution)/shard_map/all_to_all | solution.py:406
  18.2 0.0 copy-done.4
  18.2 0.0 copy-done.1
  18.2 0.0 copy-done.7
  18.2 0.0 copy-done.6
  18.2 1.3 %predict.1 = (f32[2,128]{1,0:T(2,128)}, f32[128,4,128]{2,1,0:T(4,128)S(1)}) custom-call(f32[16,40,128]{2,1,0:T(8,128)S(1)} %all_to_all.10.k_ref, s32[2,128]{1,0:T(2,128)S(1)} %bitcast.5, f32[2,128]{1,0:T(2,128)S(1)} %bitcast.6, f32[16,48,128]{2,1,0:T(8,128)S(1)} %copy-done.1, f32[4,48,128]{2,1,0:T(8,128)S(1)} %copy-done.4), custom_call_target="tpu_custom_call" | custom-call | tf_op jit(solution)/shard_map/predict/pallas_call | solution.py:407
  19.6 19.0 %all_to_all.11.got_ref = f32[128,4,128]{2,1,0:T(4,128)S(1)} all-to-all(f32[128,4,128]{2,1,0:T(4,128)S(1)} %get-tuple-element.4), channel_id=1, replica_groups=mesh['facet'=16,'col'=8] {'col','facet'}, dimensions={0} | all-to-all | bytes 524288 | tf_op jit(solution)/shard_map/all_to_all | solution.py:418
  38.5 0.0 copy-done
  38.5 0.0 copy-done.2
  38.5 0.0 copy-done.3
  38.5 0.0 copy-done.5
  38.6 7.2 %image.1 = f32[2,48,2048]{2,1,0:T(8,128)} custom-call(s32[8,16]{1,0:T(8,128)} %offset_hbm.3, f32[128,4,128]{2,1,0:T(4,128)S(1)} %all_to_all.11.got_ref, f32[16,32,128]{2,1,0:T(8,128)S(1)} %copy-done.3, bf16[8,8,96,128]{3,2,1,0:T(8,128)(2,1)S(1)} %copy-done, f32[2,16,128]{2,1,0:T(8,128)S(1)} %copy-done.5, bf16[2,256,256]{2,1,0:T(8,128)(2,1)S(1)} %copy-done.2), custom_call_target="tpu_custom_call" | custom-call | tf_op jit(solution)/shard_map/image/pallas_call | solution.py:419
Async XLA Ops:
  0.6 17.6 %copy-start.4 = (f32[4,48,128]{2,1,0:T(8,128)S(1)}, f32[4,48,128]{2,1,0:T(8,128)}, u32[]{:S(2)}) copy-start(f32[4,48,128]{2,1,0:T(8,128)} %constant.17.clone.coef_ref) | copy-start | bytes 294916
  0.6 17.6 %copy-start.1 = (f32[16,48,128]{2,1,0:T(8,128)S(1)}, f32[16,48,128]{2,1,0:T(8,128)}, u32[]{:S(2)}) copy-start(f32[16,48,128]{2,1,0:T(8,128)} %constant.16.clone.rows_ref) | copy-start | bytes 1179652
  0.7 17.5 %copy-start.7 = (f32[1,1,2,128]{3,2,1,0:T(2,128)S(1)}, f32[1,1,2,128]{3,2,1,0:T(2,128)}, u32[]{:S(2)}) copy-start(f32[1,1,2,128]{3,2,1,0:T(2,128)} %param.14) | copy-start | bytes 3076
  0.7 17.5 %copy-start.6 = (s32[1,1,2,128]{3,2,1,0:T(2,128)S(1)}, s32[1,1,2,128]{3,2,1,0:T(2,128)}, u32[]{:S(2)}) copy-start(s32[1,1,2,128]{3,2,1,0:T(2,128)} %param.13) | copy-start | bytes 3076
  0.7 37.9 %copy-start = (bf16[8,8,96,128]{3,2,1,0:T(8,128)(2,1)S(1)}, bf16[8,8,96,128]{3,2,1,0:T(8,128)(2,1)}, u32[]{:S(2)}) copy-start(bf16[8,8,96,128]{3,2,1,0:T(8,128)(2,1)} %constant.19.clone.gamma_ref) | copy-start | bytes 4718596
  0.7 37.9 %copy-start.2 = (bf16[2,256,256]{2,1,0:T(8,128)(2,1)S(1)}, bf16[2,256,256]{2,1,0:T(8,128)(2,1)}, u32[]{:S(2)}) copy-start(bf16[2,256,256]{2,1,0:T(8,128)(2,1)} %constant.20.clone.b_ref) | copy-start | bytes 786436
  0.7 37.8 %copy-start.3 = (f32[16,32,128]{2,1,0:T(8,128)S(1)}, f32[16,32,128]{2,1,0:T(8,128)}, u32[]{:S(2)}) copy-start(f32[16,32,128]{2,1,0:T(8,128)} %constant.18.clone.live_ref) | copy-start | bytes 786436
  0.7 37.8 %copy-start.5 = (f32[2,16,128]{2,1,0:T(8,128)S(1)}, f32[2,16,128]{2,1,0:T(8,128)}, u32[]{:S(2)}) copy-start(f32[2,16,128]{2,1,0:T(8,128)} %constant.14.clone.tw_hbm.tw_ref) | copy-start | bytes 49156

commit v6 on v5

--- a/solution.py
+++ b/solution.py
@@ -266,16 +266,19 @@
     fetch = pltpu.make_async_copy(offset_hbm, offset_ref, sem.at[6])
     fetch.start()
     facet, column = lax.axis_index("facet"), lax.axis_index("col")
-    grid[...] = jnp.zeros((3, PADDED, 128), F32)
+    grid[...] = jnp.zeros((3, PADDED, 2 * WIDTH), F32)
     iota = lax.broadcasted_iota(jnp.int32, (16, 128), 0)
     kap = (iota + 16 * facet).astype(F32)
     cot = live_ref[facet]
     square = 1.0 + cot * cot
     one_h = jnp.where(iota == 0, 1.0, 0.0).astype(BF16)
     none_h = jnp.zeros((32, 128), BF16)
-    pad = jnp.zeros((64 - WIDTH, 128), F32)
-    lanes = lax.broadcasted_iota(jnp.int32, (1, 128), 1)
-    turn = jnp.where(lanes < 64, -1.0, 1.0)
+    lanes = lax.broadcasted_iota(jnp.int32, (1, 2 * WIDTH), 1)
+    turn = jnp.where(lanes < WIDTH, -1.0, 1.0)
+
+    def swap(x):
+        return turn * jnp.concatenate([x[:, WIDTH:], x[:, :WIDTH]], axis=1)
+
 
     def parts(angle, cell):
         hi, lo = split(ratio(cot, square, angle))
@@ -306,7 +309,7 @@
         def columns_of(n):
             rr, ri = gots[n][0], gots[n][1]
             gr, gi = gs[n][:WIDTH], gs[n][WIDTH:]
-            w = jnp.concatenate([gr * rr - gi * ri, pad, gr * ri + gi * rr, pad], axis=0)
+            w = jnp.concatenate([gr * rr - gi * ri, gr * ri + gi * rr], axis=0)
             wh, wl = split(w)
             vh, vl = vs[n]
             left = jnp.concatenate(
@@ -316,7 +319,7 @@
 
         def place(n):
             h = hs[n]
-            total = turn * pltpu.roll(h[WIDTH : WIDTH + 1], 64, 1)
+            total = swap(h[WIDTH : WIDTH + 1])
             o = offset_ref[first + n // FACETS, n % FACETS]
             for m in range(3):
                 add = h[16 * m : 16 * m + 16]
@@ -337,12 +340,12 @@
     for row in range(0, LENGTH, 64):
         one, two, nil = (grid[m, row : row + 64, :] for m in range(3))
         d = (SUBGRID * q) * nil + (q * math.sqrt(3) / 4) * (one - two)
-        grid[2, row : row + 64, :] = d - (0.75 * q) * turn * pltpu.roll(one + two, 64, 1)
+        grid[2, row : row + 64, :] = d - (0.75 * q) * swap(one + two)
     right = (b_ref[0], b_ref[1])
     lefts = []
     for beta in range(16):
         d = grid[2, pl.ds(beta, 128, stride=16), :].T
-        lefts.append(split(jnp.concatenate([d[0:WIDTH], d[64 : 64 + WIDTH]], axis=1)))
+        lefts.append(split(jnp.concatenate([d[0:WIDTH], d[WIDTH:]], axis=1)))
     freqs = [dot3(left, right) for left in lefts]
     for beta in range(16):
         yr, yi = freqs[beta][:, :128], freqs[beta][:, 128:]
@@ -422,7 +425,7 @@
             in_specs=[hbm, vm, vm, vm, vm, vm],
             out_specs=pl.BlockSpec(memory_space=pl.ANY),
             scratch_shapes=[
-                pltpu.VMEM((3, PADDED, 128), F32),
+                pltpu.VMEM((3, PADDED, 2 * WIDTH), F32),
                 pltpu.VMEM((16, WIDTH, 256), F32),
                 pltpu.VMEM((2, WIDTH, LENGTH), F32),
                 pltpu.SMEM((COLS, FACETS), jnp.int32),

time: 46 us -> 45.8 us (level)
  no operation moved by 1% of the time
where the time goes in v6:
time: 45.8 us; the launch traced here: 45.6 us
  blocking collectives  34 us (74%)
  Pallas kernels  10.8 us (24%)
  between operations  0.73 us (2%)
    all_to_all x1, blocking collectives, body(): lax.all_to_all(send, ('col', 'facet'), split_axis=0, concat_axis=0, tiled...  19 us
    all_to_all x1, blocking collectives, body(): lax.all_to_all(windows, 'facet', split_axis=0, concat_axis=0, tiled=True)  15 us
    pallas_call x1, Pallas kernels, body(): pl.pallas_call(image_kernel, out_shape=jax.ShapeDtypeStruct((2, WIDTH, LE...  7.01 us
    pallas_call x1, Pallas kernels, body(): pl.pallas_call(extract_kernel, out_shape=jax.ShapeDtypeStruct((FACETS, SE...  2.48 us
    pallas_call x1, Pallas kernels, body(): pl.pallas_call(predict_kernel, out_shape=(jax.ShapeDtypeStruct((2, 128),...  1.35 us

profile of v6, /device:TPU:1, one launch (start us, length us, event | category | flops | bytes accessed | tf_op | source)
XLA Modules:
  0.0 45.6 jit_solution(15122301106584056175)
XLA Ops:
  0.6 0.0 copy-start.4
  0.6 0.0 copy-start.1
  0.7 0.0 copy-start.7
  0.7 0.0 copy-start.6
  0.7 0.0 copy-start
  0.7 0.0 copy-start.2
  0.7 0.0 copy-start.3
  0.7 0.0 copy-start.5
  0.7 2.5 %extract.1 = f32[16,40,128]{2,1,0:T(8,128)S(1)} custom-call(s32[8,16]{1,0:T(8,128)} %offset_hbm.3, f32[2,48,2048]{2,1,0:T(8,128)} %bitcast.7, f32[2,16,128]{2,1,0:T(8,128)} %constant.14.clone.tw_hbm.tw_ref, bf16[2,128,256]{2,1,0:T(8,128)(2,1)} %constant.15.clone.f_hbm), custom_call_target="tpu_custom_call" | custom-call | tf_op jit(solution)/shard_map/extract/pallas_call | solution.py:392
  3.2 15.0 %all_to_all.10.k_ref = f32[16,40,128]{2,1,0:T(8,128)S(1)} all-to-all(f32[16,40,128]{2,1,0:T(8,128)S(1)} %extract.1), channel_id=1, replica_groups=mesh['facet'=16,'col'=8] {'facet'}, dimensions={0} | all-to-all | bytes 655360 | tf_op jit(solution)/shard_map/all_to_all | solution.py:409
  18.2 0.0 copy-done.4
  18.2 0.0 copy-done.1
  18.2 0.0 copy-done.7
  18.2 0.0 copy-done.6
  18.2 1.3 %predict.1 = (f32[2,128]{1,0:T(2,128)}, f32[128,4,128]{2,1,0:T(4,128)S(1)}) custom-call(f32[16,40,128]{2,1,0:T(8,128)S(1)} %all_to_all.10.k_ref, s32[2,128]{1,0:T(2,128)S(1)} %bitcast.5, f32[2,128]{1,0:T(2,128)S(1)} %bitcast.6, f32[16,48,128]{2,1,0:T(8,128)S(1)} %copy-done.1, f32[4,48,128]{2,1,0:T(8,128)S(1)} %copy-done.4), custom_call_target="tpu_custom_call" | custom-call | tf_op jit(solution)/shard_map/predict/pallas_call | solution.py:410
  19.6 19.0 %all_to_all.11.got_ref = f32[128,4,128]{2,1,0:T(4,128)S(1)} all-to-all(f32[128,4,128]{2,1,0:T(4,128)S(1)} %get-tuple-element.4), channel_id=1, replica_groups=mesh['facet'=16,'col'=8] {'col','facet'}, dimensions={0} | all-to-all | bytes 524288 | tf_op jit(solution)/shard_map/all_to_all | solution.py:421
  38.5 0.0 copy-done
  38.5 0.0 copy-done.2
  38.5 0.0 copy-done.3
  38.6 0.0 copy-done.5
  38.6 7.0 %image.1 = f32[2,48,2048]{2,1,0:T(8,128)} custom-call(s32[8,16]{1,0:T(8,128)} %offset_hbm.3, f32[128,4,128]{2,1,0:T(4,128)S(1)} %all_to_all.11.got_ref, f32[16,32,128]{2,1,0:T(8,128)S(1)} %copy-done.3, bf16[8,8,96,128]{3,2,1,0:T(8,128)(2,1)S(1)} %copy-done, f32[2,16,128]{2,1,0:T(8,128)S(1)} %copy-done.5, bf16[2,256,256]{2,1,0:T(8,128)(2,1)S(1)} %copy-done.2), custom_call_target="tpu_custom_call" | custom-call | tf_op jit(solution)/shard_map/image/pallas_call | solution.py:422
Async XLA Ops:
  0.6 17.6 %copy-start.4 = (f32[4,48,128]{2,1,0:T(8,128)S(1)}, f32[4,48,128]{2,1,0:T(8,128)}, u32[]{:S(2)}) copy-start(f32[4,48,128]{2,1,0:T(8,128)} %constant.17.clone.coef_ref) | copy-start | bytes 294916
  0.6 17.6 %copy-start.1 = (f32[16,48,128]{2,1,0:T(8,128)S(1)}, f32[16,48,128]{2,1,0:T(8,128)}, u32[]{:S(2)}) copy-start(f32[16,48,128]{2,1,0:T(8,128)} %constant.16.clone.rows_ref) | copy-start | bytes 1179652
  0.7 17.5 %copy-start.7 = (f32[1,1,2,128]{3,2,1,0:T(2,128)S(1)}, f32[1,1,2,128]{3,2,1,0:T(2,128)}, u32[]{:S(2)}) copy-start(f32[1,1,2,128]{3,2,1,0:T(2,128)} %param.14) | copy-start | bytes 3076
  0.7 17.5 %copy-start.6 = (s32[1,1,2,128]{3,2,1,0:T(2,128)S(1)}, s32[1,1,2,128]{3,2,1,0:T(2,128)}, u32[]{:S(2)}) copy-start(s32[1,1,2,128]{3,2,1,0:T(2,128)} %param.13) | copy-start | bytes 3076
  0.7 37.9 %copy-start = (bf16[8,8,96,128]{3,2,1,0:T(8,128)(2,1)S(1)}, bf16[8,8,96,128]{3,2,1,0:T(8,128)(2,1)}, u32[]{:S(2)}) copy-start(bf16[8,8,96,128]{3,2,1,0:T(8,128)(2,1)} %constant.19.clone.gamma_ref) | copy-start | bytes 4718596
  0.7 37.9 %copy-start.2 = (bf16[2,256,256]{2,1,0:T(8,128)(2,1)S(1)}, bf16[2,256,256]{2,1,0:T(8,128)(2,1)}, u32[]{:S(2)}) copy-start(bf16[2,256,256]{2,1,0:T(8,128)(2,1)} %constant.20.clone.b_ref) | copy-start | bytes 786436
  0.7 37.8 %copy-start.3 = (f32[16,32,128]{2,1,0:T(8,128)S(1)}, f32[16,32,128]{2,1,0:T(8,128)}, u32[]{:S(2)}) copy-start(f32[16,32,128]{2,1,0:T(8,128)} %constant.18.clone.live_ref) | copy-start | bytes 786436
  0.7 37.8 %copy-start.5 = (f32[2,16,128]{2,1,0:T(8,128)S(1)}, f32[2,16,128]{2,1,0:T(8,128)}, u32[]{:S(2)}) copy-start(f32[2,16,128]{2,1,0:T(8,128)} %constant.14.clone.tw_hbm.tw_ref) | copy-start | bytes 49156
